TPU v7x, 1024 devices: a whole 8x8x8 slice. The times are simulated.
1024 devices in a mesh: dom: 128 (over x_hi, z, y), band: 8 (over x_lo, core).
Axes of the slice: x: 8 (x_hi: 2, x_lo: 4; x = x_hi * 4 + x_lo), y: 8, z: 8, core: 2. Of those that a mesh axis runs over, the one named last changes fastest.
Arguments:
- filter_input: bfloat16 [165888, 2048], P('dom', 'band'), may hold values from -6 to 6
- element_matrix: bfloat16 [125, 125], replicated, as said below
- cell_scale: float32 [2048], P('dom'), may hold values from 0.5 to 2
- connectivity: int32 [2048, 125], P('dom'), may hold values from 0 to 1376, as said below
- interface_nodes: int32 [10368], P('dom'), may hold values from 0 to 1295, as said below
- lumped_mass: float32 [165888], P('dom'), may hold values from 0.5 to 2
- potential: float32 [165888], P('dom'), may hold values from -1 to 1
Outputs:
- filtered: bfloat16 [165888, 2048], P('dom', 'band')
- intersection: float32 [2048, 2048], P('dom', 'band')
Inputs may be any that keep to these rules, and one draw needn't show every extreme that they name: `connectivity`: within a cell the indices are distinct; indices of 1296 and above stand only in a domain's last 4 cells. `interface_nodes`: within one domain's list the nodes are distinct. `element_matrix`: symmetric positive definite: a sum over the three directions of degree-4 Gauss-Lobatto stiffness terms with positive factors, plus a positive diagonal mass term.
All inputs are finite; a program needn't handle non-finite values.
Results may differ from a plain program's by a relative error of at most 0.0081.
The roundings to bfloat16 on the way count: a program that leaves them out, or rounds other values in their place, can miss the bound.
Values may be sent and summed in bfloat16 or wider, within the bound.
No kernel may reach another device: no remote copies, remote signals or barrier semaphores. Data moves between devices by JAX's collectives and lax.ppermute only.
A program may use at most 32 MiB of HBM per device.

v0:
```python
import jax
import jax.numpy as jnp
from jax import lax
from jax.sharding import PartitionSpec as P

filter_center = 5.0
filter_width = 6.0


def shifted(value, axis, steps):
    count = lax.axis_size(axis)
    pairs = [(source, (source + steps) % count) for source in range(count)]
    return lax.ppermute(value, axis, pairs)


def cell_terms(rows, element_matrix, cells, scales):
    picked = rows[cells]
    products = jnp.einsum("ab,cbs->cas", element_matrix, picked, preferred_element_type=jnp.float32)
    products = products * scales[:, None, None]
    return products.reshape(-1, rows.shape[1])


def apply_operator(
    values_in, element_matrix, cell_scale, connectivity, interface_nodes, lumped_mass, potential
):
    owned_count = values_in.shape[0]
    shared_rows = values_in[interface_nodes]
    remote = shifted(shared_rows, "dom", -1)
    extended = jnp.concatenate([values_in, remote], axis=0)
    summed = jnp.zeros(extended.shape, jnp.float32)
    summed = summed.at[connectivity.reshape(-1)].add(
        cell_terms(extended, element_matrix, connectivity, cell_scale)
    )
    returned = shifted(summed[owned_count:].astype(jnp.bfloat16), "dom", 1).astype(jnp.float32)
    owned_rows = summed[:owned_count].at[interface_nodes].add(returned)
    return owned_rows / lumped_mass[:, None] + potential[:, None] * values_in.astype(jnp.float32)


def per_device(
    filter_input, element_matrix, cell_scale, connectivity, interface_nodes, lumped_mass, potential
):
    start_values = filter_input.astype(jnp.float32)
    first_image = apply_operator(
        filter_input,
        element_matrix,
        cell_scale,
        connectivity,
        interface_nodes,
        lumped_mass,
        potential,
    )
    middle = ((first_image - filter_center * start_values) / filter_width).astype(jnp.bfloat16)
    second_image = apply_operator(
        middle, element_matrix, cell_scale, connectivity, interface_nodes, lumped_mass, potential
    )
    filtered = (
        2.0 * (second_image - filter_center * middle.astype(jnp.float32)) / filter_width
        - start_values
    ).astype(jnp.bfloat16)
    domain_count = lax.axis_size("dom")
    node_total = filtered.shape[0] * domain_count
    weighted = (filtered.astype(jnp.float32) * (lumped_mass / float(node_total))[:, None]).astype(
        jnp.bfloat16
    )
    gathered = lax.all_gather(filtered, "band", axis=1, tiled=True)
    intersection = lax.psum_scatter(
        lax.dot_general(
            gathered, weighted, (((0,), (0,)), ((), ())), preferred_element_type=jnp.float32
        ),
        "dom",
        scatter_dimension=0,
        tiled=True,
    )
    return (filtered, intersection)


def solution(mesh):
    placed = (P("dom", "band"), P(), P("dom"), P("dom", None), P("dom"), P("dom"), P("dom"))
    return jax.shard_map(
        per_device,
        mesh=mesh,
        in_specs=placed,
        out_specs=(P("dom", "band"), P("dom", "band")),
        check_vma=False,
    )
```

profile of v0, /device:TPU:2, one launch (start us, length us, event | category | flops | bytes accessed | tf_op | source)
XLA Modules:
  0.0 1084.5 jit_solution(11920532630643859159)
XLA Ops:
  7.2 0.0 copy-start
  7.2 0.0 all-gather.2.cloned.1.call-start
  7.2 0.7 compare_select_fusion.2
  7.9 1.9 gather_fusion
  9.7 25.0 %collective-permute-start = (bf16[81,256]{1,0:T(8,128)(2,1)S(1)}, bf16[81,256]{1,0:T(8,128)(2,1)S(1)}, u32[]{:S(2)}, u32[]{:S(2)}) collective-permute-start(bf16[81,256]{1,0:T(8,128)(2,1)S(1)} %gather_fusion), channel_id=1, source_target_pairs={{0,1016},{8,0},{16,8},{24,16},{32,24},{40,32},{48,40},{56,48},{64,... | collective-permute-start | bytes 124424 | tf_op jit(solution)/shard_map/ppermute | solution.py:13
  34.8 0.7 compare_select_fusion.1
  35.5 0.8 reshape.46
  36.3 0.1 reshape.59
  36.4 0.4 collective-permute-done
  36.9 1.1 pad_maximum_fusion
  38.0 7.7 gather_fusion.1
  45.7 0.0 copy-start.4
  45.7 0.3 reshape.58
  46.0 0.0 copy-done
  46.0 0.3 copy-done.4
  46.3 0.4 multiply_bitcast_fusion.1
  46.8 1.6 reshape.85
  48.4 11.3 %scatter_custom_fusion = f32[1377,256]{1,0:T(8,128)S(1)} fusion(s32[2000]{0:T(1024)S(1)} %bitcast.13, f32[2000,256]{1,0:T(8,128)} %reshape.85, f32[]{:T(128)} %constant.8.clone.1), kind=kCustom, calls=%fused_computation.28 | custom fusion | flops 512000 | bytes 1410560 | tf_op jit(solution)/shard_map/scatter-add | solution.py:31
  59.6 0.0 copy-start.1
  59.7 0.0 copy-start.2
  59.7 0.0 copy-start.3
  59.7 2.1 collective-permute-start.1
  61.7 0.1 slice.26
  61.8 12.7 %collective-permute-done.1 = bf16[81,256]{1,0:T(8,128)(2,1)S(1)} collective-permute-done((bf16[81,256]{1,0:T(8,128)(2,1)S(1)}, bf16[81,256]{1,0:T(8,128)(2,1)S(1)}, u32[]{:S(2)}, u32[]{:S(2)}) %collective-permute-start.1) | collective-permute-done | bytes 41504 | tf_op jit(solution)/shard_map/ppermute | solution.py:13
  74.5 1.5 scatter_custom_fusion.1
  76.0 0.0 copy-done.1
  76.1 0.0 copy-done.2
  76.1 0.0 copy-done.3
  76.1 0.4 fusion.6
  76.5 0.7 gather_fusion.2
  77.3 3.7 collective-permute-start.2
  81.0 2.2 collective-permute-done.2
  83.2 0.1 pad_maximum_fusion.1
  83.2 7.7 gather_fusion.3
  90.9 1.3 reshape.74
  92.2 1.6 multiply_bitcast_fusion
  93.9 1.6 reshape.101
  95.5 11.3 %scatter_custom_fusion.2 = f32[1377,256]{1,0:T(8,128)S(1)} fusion(s32[2000]{0:T(1024)S(1)} %bitcast.14, f32[2000,256]{1,0:T(8,128)} %reshape.101, f32[]{:T(128)} %constant.8.clone.1), kind=kCustom, calls=%fused_computation.26 | custom fusion | flops 512000 | bytes 1410560 | tf_op jit(solution)/shard_map/scatter-add | solution.py:31
  106.8 1.9 collective-permute-start.3
  108.7 1.2 slice.28
  109.8 11.0 %collective-permute-done.3 = bf16[81,256]{1,0:T(8,128)(2,1)S(1)} collective-permute-done((bf16[81,256]{1,0:T(8,128)(2,1)S(1)}, bf16[81,256]{1,0:T(8,128)(2,1)S(1)}, u32[]{:S(2)}, u32[]{:S(2)}) %collective-permute-start.3) | collective-permute-done | bytes 41504 | tf_op jit(solution)/shard_map/ppermute | solution.py:13
  120.8 3.3 scatter_custom_fusion.3
  124.2 2.7 fusion.7
  126.9 0.0 all-gather.2.cloned.1.call-update
  126.9 0.0 reduce-scatter.2.cloned.1.call-start
  127.0 54.9 %all-gather.2.cloned.1.call-done = bf16[1296,2048]{1,0:T(8,128)(2,1)} async-done(((bf16[1296,256]{1,0:T(8,128)(2,1)}), bf16[1296,2048]{1,0:T(8,128)(2,1)}) %all-gather.2.cloned.1.call-update) | async-done | bytes 5308432 | tf_op jit(solution)/shard_map/all_gather | solution.py:65
  181.9 6.1 fusion.12
  188.0 0.0 reduce-scatter.2.cloned.1.call-update
  188.0 889.6 %reduce-scatter.2.cloned.1.call-done = f32[16,256]{1,0:T(8,128)} async-done(((f32[2048,256]{1,0:T(8,128)}), f32[16,256]{1,0:T(8,128)}) %reduce-scatter.2.cloned.1.call-update) | async-done | bytes 16400 | tf_op jit(solution)/shard_map/reduce_scatter | solution.py:66
  (6 shorter events, 0.0 us)
Async XLA Ops:
  7.2 38.8 %copy-start = (bf16[125,125]{1,0:T(8,128)(2,1)S(1)}, bf16[125,125]{1,0:T(8,128)(2,1)}, u32[]{:S(2)}) copy-start(bf16[125,125]{1,0:T(8,128)(2,1)} %param.8) | copy-start | bytes 93754
  7.2 174.7 %all-gather.2.cloned.1.call-start = ((), (), s32[]{:S(2)}) async-start(), calls=%async_computation.1 | async-start | bytes 5971968 | tf_op jit(solution)/shard_map/all_gather | solution.py:65
  9.7 27.1 %collective-permute-start = (bf16[81,256]{1,0:T(8,128)(2,1)S(1)}, bf16[81,256]{1,0:T(8,128)(2,1)S(1)}, u32[]{:S(2)}, u32[]{:S(2)}) collective-permute-start(bf16[81,256]{1,0:T(8,128)(2,1)S(1)} %gather_fusion), channel_id=1, source_target_pairs={{0,1016},{8,0},{16,8},{24,16},{32,24},{40,32},{48,40},{56,48},{64,... | collective-permute-start | bytes 124424 | tf_op jit(solution)/shard_map/ppermute | solution.py:13
  45.7 0.7 copy-start.4
  59.6 16.4 %copy-start.1 = (bf16[1296,256]{1,0:T(8,128)(2,1)S(1)}, bf16[1296,256]{1,0:T(8,128)(2,1)}, u32[]{:S(2)}) copy-start(bf16[1296,256]{1,0:T(8,128)(2,1)} %param.7) | copy-start | bytes 1990660
  59.7 16.4 %copy-start.2 = (f32[1296]{0:T(1024)S(1)}, f32[1296]{0:T(1024)}, u32[]{:S(2)}) copy-start(f32[1296]{0:T(1024)} %param.12) | copy-start | bytes 15556
  59.7 16.4 %copy-start.3 = (f32[1296]{0:T(1024)S(1)}, f32[1296]{0:T(1024)}, u32[]{:S(2)}) copy-start(f32[1296]{0:T(1024)} %param.13) | copy-start | bytes 15556
  59.7 14.9 %collective-permute-start.1 = (bf16[81,256]{1,0:T(8,128)(2,1)S(1)}, bf16[81,256]{1,0:T(8,128)(2,1)S(1)}, u32[]{:S(2)}, u32[]{:S(2)}) collective-permute-start(bf16[81,256]{1,0:T(8,128)(2,1)S(1)} %slice.33), channel_id=1, source_target_pairs={{0,8},{8,16},{16,24},{24,32},{32,40},{40,48},{48,56},{56,64},{64,7... | collective-permute-start | bytes 124424 | tf_op jit(solution)/shard_map/ppermute | solution.py:13
  77.3 5.9 collective-permute-start.2
  106.8 14.1 %collective-permute-start.3 = (bf16[81,256]{1,0:T(8,128)(2,1)S(1)}, bf16[81,256]{1,0:T(8,128)(2,1)S(1)}, u32[]{:S(2)}, u32[]{:S(2)}) collective-permute-start(bf16[81,256]{1,0:T(8,128)(2,1)S(1)} %slice.32), channel_id=1, source_target_pairs={{0,8},{8,16},{16,24},{24,32},{32,40},{40,48},{48,56},{56,64},{64,7... | collective-permute-start | bytes 124424 | tf_op jit(solution)/shard_map/ppermute | solution.py:13
  126.9 950.8 %reduce-scatter.2.cloned.1.call-start = ((), (), s32[]{:S(2)}) async-start(), calls=%async_computation.2 | async-start | bytes 2113536 | tf_op jit(solution)/shard_map/reduce_scatter | solution.py:66
Sparse Core Ops, SparseCore 0:
  127.0 54.8 all-gather.1
  188.1 889.4 reduce-scatter.1
where the time goes:
time: 1090 us; the launch traced here: 1080 us
  waiting for transfers between devices  971 us (89%)
  other arithmetic  33.1 us (3%)
  starting transfers between devices  32.8 us (3%)
  local copies, waits for them, and re-layouts  25.2 us (2%)
  between operations  14.3 us (1%)
    reduce_scatter x1, waiting for transfers between devices, per_device(): lax.psum_scatter(lax.dot_general(gathered, weighted, (((0,), (0,)), ((),...  890 us
    all_gather x1, waiting for transfers between devices, per_device(): gathered = lax.all_gather(filtered, 'band', axis=1, tiled=True)  54.9 us
    ppermute x4, starting transfers between devices, shifted(): return lax.ppermute(value, axis, pairs)  32.7 us
    ppermute x4, waiting for transfers between devices, shifted(): return lax.ppermute(value, axis, pairs)  26.4 us
    scatter-add x2, other arithmetic, apply_operator(): summed.at[connectivity.reshape(-1)]  22.5 us
  transfers between devices with their start and end apart: 6, of which 6 were waited for; matrix products, arithmetic and copies ran while one was open for 0% of the time, Pallas kernels for 0%

commit v1 on v0

v1 whole, which is shorter than its diff:
```python
import jax
import jax.numpy as jnp
from jax import lax
from jax.experimental import pallas as pl
from jax.experimental.pallas import tpu as pltpu
from jax.sharding import PartitionSpec as P

filter_center = 5.0
filter_width = 6.0

OWN = 1296
SHARED = 81
CELLS = 16
NPC = 125
STATES_DEV = 256
PAD = 128
OWN_PAD = 1408
INNER = 12
ENTRIES = CELLS * PAD
INNER_ENTRIES = INNER * PAD
OUTER_ENTRIES = ENTRIES - INNER_ENTRIES
IFACE_SLOT = 16
SLOTS = 24
BF = jnp.bfloat16
F32 = jnp.float32


def shifted(value, axis, steps):
    count = lax.axis_size(axis)
    pairs = [(source, (source + steps) % count) for source in range(count)]
    return lax.ppermute(value, axis, pairs)


def rows_match(column, width):
    lanes = lax.broadcasted_iota(jnp.int32, (column.shape[0], width), 1)
    return jnp.where(lanes == column, 1.0, 0.0).astype(BF)


def columns_match(row, start, height):
    places = lax.broadcasted_iota(jnp.int32, (height, row.shape[1]), 0)
    return jnp.where(places == row - start, 1.0, 0.0).astype(BF)


def dot(left, right):
    return jnp.dot(left, right, preferred_element_type=F32)


def two_parts(value):
    high = value.astype(BF)
    low = (value - high.astype(F32)).astype(BF)
    return high, low


def cell_products(gathered, element_ref, scale_ref, first_cell, out_ref, out_start):
    for pair in range(gathered.shape[0] // (2 * PAD)):
        block = gathered[pair * 2 * PAD : (pair + 1) * 2 * PAD]
        products = dot(element_ref[...], block)
        for half in range(2):
            scale = scale_ref[first_cell + 2 * pair + half]
            high, low = two_parts(products[half * PAD : (half + 1) * PAD] * scale)
            start = out_start + (2 * pair + half) * PAD
            out_ref[start : start + PAD, :STATES_DEV] = high
            out_ref[start : start + PAD, STATES_DEV:] = low


def inner_kernel(scale_ref, values_ref, index_t_ref, element_ref, terms_ref, outer_ref, padded, match):
    padded[:OWN, :] = values_ref[...]
    padded[OWN:, :] = jnp.zeros((OWN_PAD - OWN, STATES_DEV), BF)
    for group in range(4):
        for cell in range(4):
            number = group * 4 + cell
            match[cell * PAD : (cell + 1) * PAD, :] = rows_match(
                index_t_ref[:, number : number + 1], OWN_PAD
            )
        gathered = dot(match[...], padded[...]).astype(BF)
        if group < 3:
            cell_products(gathered, element_ref, scale_ref, group * 4, terms_ref, group * 4 * PAD)
        else:
            outer_ref[...] = gathered


def outer_kernel(
    scale_ref, outer_ref, remote_ref, index_ref, index_t_ref, element_ref, terms_ref, back_ref, held
):
    held[...] = jnp.zeros_like(held)
    held[:SHARED, :] = remote_ref[...]
    match = jnp.concatenate(
        [
            rows_match(index_t_ref[:, INNER + cell : INNER + cell + 1] - OWN, PAD)
            for cell in range(CELLS - INNER)
        ],
        axis=0,
    )
    gathered = (outer_ref[...].astype(F32) + dot(match, held[...])).astype(BF)
    cell_products(gathered, element_ref, scale_ref, INNER, terms_ref, 0)
    match = jnp.concatenate(
        [
            columns_match(index_ref[INNER + cell : INNER + cell + 1, :], OWN, PAD)
            for cell in range(CELLS - INNER)
        ],
        axis=1,
    )
    both = dot(match, terms_ref[...])
    back = (both[:, :STATES_DEV] + both[:, STATES_DEV:]).astype(BF)
    back_ref[...] = back[:SHARED, :]


def spread_kernel(inner_ref, outer_ref, index_ref, summed_ref, match):
    step = OWN // 3
    for tile in range(3):
        for cell in range(CELLS):
            match[:, cell * PAD : (cell + 1) * PAD] = columns_match(
                index_ref[cell : cell + 1, :], tile * step, step
            )
        both = dot(match[:, :INNER_ENTRIES], inner_ref[...]) + dot(
            match[:, INNER_ENTRIES:], outer_ref[...]
        )
        summed_ref[tile * step : (tile + 1) * step, :] = (
            both[:, :STATES_DEV] + both[:, STATES_DEV:]
        )


def with_returned(summed_ref, back_ref, index_ref, held):
    held[...] = jnp.zeros_like(held)
    held[:SHARED, :] = back_ref[...]
    match = columns_match(index_ref[IFACE_SLOT : IFACE_SLOT + 1, :], 0, OWN)
    return summed_ref[...] + dot(match, held[...])


def middle_kernel(
    summed_ref,
    back_ref,
    values_ref,
    mass_ref,
    potential_ref,
    index_ref,
    index_t_ref,
    middle_ref,
    shared_ref,
    held,
    padded,
):
    summed = with_returned(summed_ref, back_ref, index_ref, held)
    factor = 1.0 / (filter_width * mass_ref[...])
    own = (potential_ref[...] - filter_center) * (1.0 / filter_width)
    middle = (summed * factor + values_ref[...].astype(F32) * own).astype(BF)
    middle_ref[...] = middle
    padded[:OWN, :] = middle
    padded[OWN:, :] = jnp.zeros((OWN_PAD - OWN, STATES_DEV), BF)
    match = rows_match(index_t_ref[:, IFACE_SLOT : IFACE_SLOT + 1], OWN_PAD)
    shared_ref[...] = dot(match, padded[...]).astype(BF)[:SHARED, :]


def final_kernel(
    total_ref,
    summed_ref,
    back_ref,
    middle_ref,
    values_ref,
    mass_ref,
    potential_ref,
    index_ref,
    filtered_ref,
    weighted_ref,
    held,
):
    summed = with_returned(summed_ref, back_ref, index_ref, held)
    mass = mass_ref[...]
    factor = (2.0 / filter_width) / mass
    own = (potential_ref[...] - filter_center) * (2.0 / filter_width)
    filtered = (
        summed * factor + middle_ref[...].astype(F32) * own - values_ref[...].astype(F32)
    ).astype(BF)
    filtered_ref[...] = filtered
    weighted_ref[...] = (filtered.astype(F32) * (mass * total_ref[0])).astype(BF)


SCALARS = pl.BlockSpec(memory_space=pltpu.SMEM)
ARRAY = pl.BlockSpec(memory_space=pltpu.VMEM)
LIMIT = 40 * 1024 * 1024


def call(body, scalars, arrays, outs, scratch, flops, *args):
    return pl.pallas_call(
        body,
        out_shape=outs,
        in_specs=[SCALARS] * scalars + [ARRAY] * arrays,
        out_specs=[ARRAY] * len(outs),
        scratch_shapes=scratch,
        compiler_params=pltpu.CompilerParams(vmem_limit_bytes=LIMIT),
        cost_estimate=pl.CostEstimate(flops=flops, bytes_accessed=3_000_000, transcendentals=0),
    )(*args)


def shape(rows, columns, dtype):
    return jax.ShapeDtypeStruct((rows, columns), dtype)


def summed_terms(values, shared, scales, index, index_t, element):
    remote = shifted(shared, "dom", -1)
    inner, outer = call(
        inner_kernel,
        1,
        3,
        [shape(INNER_ENTRIES, 2 * STATES_DEV, BF), shape(OUTER_ENTRIES, STATES_DEV, BF)],
        [pltpu.VMEM((OWN_PAD, STATES_DEV), BF), pltpu.VMEM((4 * PAD, OWN_PAD), BF)],
        1_600_000_000,
        scales,
        values,
        index_t,
        element,
    )
    outer_terms, back = call(
        outer_kernel,
        1,
        5,
        [shape(OUTER_ENTRIES, 2 * STATES_DEV, BF), shape(SHARED, STATES_DEV, BF)],
        [pltpu.VMEM((PAD, STATES_DEV), BF)],
        200_000_000,
        scales,
        outer,
        remote,
        index,
        index_t,
        element,
    )
    returned = shifted(back, "dom", 1)
    (summed,) = call(
        spread_kernel,
        0,
        3,
        [shape(OWN, STATES_DEV, F32)],
        [pltpu.VMEM((OWN // 3, ENTRIES), BF)],
        2_700_000_000,
        inner,
        outer_terms,
        index,
    )
    return summed, returned


def filtered_states(
    filter_input, element_matrix, cell_scale, connectivity, interface_nodes, lumped_mass, potential
):
    shared = filter_input[interface_nodes]
    index = jnp.full((SLOTS, PAD), -1, jnp.int32)
    index = index.at[:CELLS, :NPC].set(connectivity)
    index = index.at[IFACE_SLOT, :SHARED].set(interface_nodes)
    index_t = index.T
    element = jnp.zeros((2 * PAD, 2 * PAD), BF)
    element = element.at[:NPC, :NPC].set(element_matrix)
    element = element.at[PAD : PAD + NPC, PAD : PAD + NPC].set(element_matrix)
    mass = lumped_mass[:, None]
    pot = potential[:, None]
    summed, returned = summed_terms(filter_input, shared, cell_scale, index, index_t, element)
    middle, shared = call(
        middle_kernel,
        0,
        7,
        [shape(OWN, STATES_DEV, BF), shape(SHARED, STATES_DEV, BF)],
        [pltpu.VMEM((PAD, STATES_DEV), BF), pltpu.VMEM((OWN_PAD, STATES_DEV), BF)],
        200_000_000,
        summed,
        returned,
        filter_input,
        mass,
        pot,
        index,
        index_t,
    )
    summed, returned = summed_terms(middle, shared, cell_scale, index, index_t, element)
    node_total = OWN * lax.axis_size("dom")
    total = jnp.full((1,), 1.0 / float(node_total), F32)
    return call(
        final_kernel,
        1,
        7,
        [shape(OWN, STATES_DEV, BF), shape(OWN, STATES_DEV, BF)],
        [pltpu.VMEM((PAD, STATES_DEV), BF)],
        200_000_000,
        total,
        summed,
        returned,
        middle,
        filter_input,
        mass,
        pot,
        index,
    )


def per_device(*args):
    filtered, weighted = filtered_states(*args)
    gathered = lax.all_gather(filtered, "band", axis=1, tiled=True)
    terms = lax.dot_general(
        gathered, weighted, (((0,), (0,)), ((), ())), preferred_element_type=jnp.float32
    ).astype(BF)
    domains = lax.axis_size("dom")
    pieces = lax.all_to_all(terms.reshape(domains, -1, terms.shape[1]), "dom", 0, 0)
    return filtered, jnp.sum(pieces.astype(F32), axis=0)


def solution(mesh):
    placed = (P("dom", "band"), P(), P("dom"), P("dom", None), P("dom"), P("dom"), P("dom"))
    return jax.shard_map(
        per_device,
        mesh=mesh,
        in_specs=placed,
        out_specs=(P("dom", "band"), P("dom", "band")),
        check_vma=False,
    )
```

time: 1090 us -> 211 us (0.19)
  waiting for transfers between devices: 971 us -> 71.1 us
  blocking collectives: 0 us -> 56.5 us
  other arithmetic: 33.1 us -> 1.47 us
  Pallas kernels: 0 us -> 21.9 us
  local copies, waits for them, and re-layouts: 25.2 us -> 8.09 us
    reduce_scatter x1 -> x0, waiting for transfers between devices: 890 us -> none  [per_device(): lax.psum_scatter(lax.dot_general(gathered, weighted, (((0,), (0,)), ((),...]
    all_to_all x0 -> x1, blocking collectives: none -> 56.5 us  [per_device(): lax.all_to_all(terms.reshape(domains, -1, terms.shape[1]), 'dom', 0, 0)]
    scatter-add x4 -> x0, other arithmetic: 27.3 us -> none  [the longest x2 22.5 us: apply_operator(): summed.at[connectivity.reshape(-1)]]
    pallas_call x0 -> x8, Pallas kernels: none -> 21.9 us  [call(): pl.pallas_call(body, out_shape=outs, in_specs=[SCALARS] * scalars + [ARRA...]
    gather x6 -> x1, local copies, waits for them, and re-layouts: 19.6 us -> 1.85 us  [filtered_states(): shared = filter_input[interface_nodes]]
  transfers between devices with their start and end apart: 6 -> 5, of which waited for: 6 -> 3; matrix products, arithmetic and copies ran while one was open for 0% -> 2% of each run, Pallas kernels for 0% -> 8%
where the time goes in v1:
time: 211 us
  waiting for transfers between devices  71.1 us (34%)
  blocking collectives  56.5 us (27%)
  starting transfers between devices  33 us (16%)
  Pallas kernels  21.9 us (10%)
  between operations  14.2 us (7%)
  local copies, waits for them, and re-layouts  8.09 us (4%)
  matrix products  4.38 us (2%)
    all_to_all x1, blocking collectives, per_device(): lax.all_to_all(terms.reshape(domains, -1, terms.shape[1]), 'dom', 0, 0)  56.5 us
    all_gather x1, waiting for transfers between devices, per_device(): gathered = lax.all_gather(filtered, 'band', axis=1, tiled=True)  54.1 us
    ppermute x4, starting transfers between devices, shifted(): return lax.ppermute(value, axis, pairs)  33 us
    pallas_call x8, Pallas kernels, call(): pl.pallas_call(body, out_shape=outs, in_specs=[SCALARS] * scalars + [ARRA...  21.9 us
    ppermute x4, waiting for transfers between devices, shifted(): return lax.ppermute(value, axis, pairs)  17 us
    dot_general x1, matrix products, per_device(): lax.dot_general(gathered, weighted, (((0,), (0,)), ((), ())), preferred_e...  4.38 us
  transfers between devices with their start and end apart: 5, of which 3 were waited for; matrix products, arithmetic and copies ran while one was open for 2% of the time, Pallas kernels for 8%

profile of v1, /device:TPU:2, one launch (start us, length us, event | category | flops | bytes accessed | tf_op | source)
XLA Modules:
  0.0 210.6 jit_solution(14045064081414375695)
XLA Ops:
  7.2 0.0 all-gather.2.cloned.1.call-start
  7.2 0.7 compare_select_fusion
  7.9 1.9 gather_fusion
  9.7 25.0 %collective-permute-start = (bf16[81,256]{1,0:T(8,128)(2,1)S(1)}, bf16[81,256]{1,0:T(8,128)(2,1)S(1)}, u32[]{:S(2)}, u32[]{:S(2)}) collective-permute-start(bf16[81,256]{1,0:T(8,128)(2,1)S(1)} %gather_fusion), channel_id=1, source_target_pairs={{0,1016},{8,0},{16,8},{24,16},{32,24},{40,32},{48,40},{56,48},{64,... | collective-permute-start | bytes 124424 | tf_op jit(solution)/shard_map/ppermute | solution.py:31
  34.8 0.7 scatter.14
  35.5 0.7 scatter.15.index_ref
  36.2 0.1 copy.14.index_t_ref
  36.3 0.8 scatter.16
  37.1 1.7 scatter.19.element_ref
  38.8 0.0 copy-start
  38.8 1.1 copy-done
  39.9 0.0 copy-start.2
  39.9 0.7 copy-done.2
  40.6 0.0 copy-start.4
  40.6 0.0 copy-start.5
  40.6 4.8 %shard_map.86 = (bf16[1536,512]{1,0:T(8,128)(2,1)S(1)}, bf16[512,256]{1,0:T(8,128)(2,1)S(1)}) custom-call(f32[16]{0:T(128)S(1)} %copy-done.2, bf16[1296,256]{1,0:T(8,128)(2,1)S(1)} %copy-done, s32[128,24]{1,0:T(8,128)S(1)} %copy.14.index_t_ref, bf16[256,256]{1,0:T(8,128)(2,1)S(1)} %scatter.19.element_ref), custom_call_target="tpu_custom_call" | custom-call | flops 1600000000 | bytes 3000000 | tf_op jit(solution)/shard_map/pallas_call | solution.py:184
  45.4 0.0 copy-done.4
  45.4 0.2 broadcast_in_dim.14.mass_ref
  45.7 0.0 copy-done.5
  45.7 0.2 broadcast_in_dim.15.potential_ref
  45.9 0.0 collective-permute-done.remote_ref
  45.9 1.3 shard_map.87
  47.2 1.9 collective-permute-start.1
  49.1 0.0 copy-start.1
  49.1 3.6 %shard_map.88.summed_ref = f32[1296,256]{1,0:T(8,128)S(1)} custom-call(bf16[1536,512]{1,0:T(8,128)(2,1)S(1)} %get-tuple-element.62.inner_ref, bf16[512,512]{1,0:T(8,128)(2,1)S(1)} %get-tuple-element.64.outer_ref, s32[24,128]{1,0:T(8,128)S(1)} %scatter.15.index_ref), custom_call_target="tpu_custom_call" | custom-call | flops 2700000000 | bytes 3000000 | tf_op jit(solution)/shard_map/pallas_call | solution.py:184
  52.8 0.0 copy-start.3
  52.8 9.0 %collective-permute-done.1.back_ref = bf16[81,256]{1,0:T(8,128)(2,1)S(1)} collective-permute-done((bf16[81,256]{1,0:T(8,128)(2,1)S(1)}, bf16[81,256]{1,0:T(8,128)(2,1)S(1)}, u32[]{:S(2)}, u32[]{:S(2)}) %collective-permute-start.1) | collective-permute-done | bytes 41504 | tf_op jit(solution)/shard_map/ppermute | solution.py:31
  61.7 0.0 copy-done.1
  61.8 0.8 shard_map.89
  62.6 3.1 %collective-permute-start.2 = (bf16[81,256]{1,0:T(8,128)(2,1)S(1)}, bf16[81,256]{1,0:T(8,128)(2,1)S(1)}, u32[]{:S(2)}, u32[]{:S(2)}) collective-permute-start(bf16[81,256]{1,0:T(8,128)(2,1)S(1)} %get-tuple-element.69), channel_id=1, source_target_pairs={{0,1016},{8,0},{16,8},{24,16},{32,24},{40,32},{48,40},{56,48},{64,... | collective-permute-start | bytes 124424 | tf_op jit(solution)/shard_map/ppermute | solution.py:31
  65.7 0.0 copy-done.3
  65.7 4.8 %shard_map.90 = (bf16[1536,512]{1,0:T(8,128)(2,1)S(1)}, bf16[512,256]{1,0:T(8,128)(2,1)S(1)}) custom-call(f32[16]{0:T(128)S(1)} %copy-done.3, bf16[1296,256]{1,0:T(8,128)(2,1)S(1)} %get-tuple-element.66.values_ref.middle_ref, s32[128,24]{1,0:T(8,128)S(1)} %copy.14.index_t_ref, bf16[256,256]{1,0:T(8,128)(2,1)S(1)} %scatter.19.element_ref), custom_call_target="tpu_custom_call" | custom-call | flops 1600000000 | bytes 3000000 | tf_op jit(solution)/shard_map/pallas_call | solution.py:184
  70.5 0.0 collective-permute-done.2.remote_ref
  70.5 1.3 shard_map.91
  71.8 2.9 %collective-permute-start.3 = (bf16[81,256]{1,0:T(8,128)(2,1)S(1)}, bf16[81,256]{1,0:T(8,128)(2,1)S(1)}, u32[]{:S(2)}, u32[]{:S(2)}) collective-permute-start(bf16[81,256]{1,0:T(8,128)(2,1)S(1)} %get-tuple-element.71), channel_id=1, source_target_pairs={{0,8},{8,16},{16,24},{24,32},{32,40},{40,48},{48,56},{56,64},{64,7... | collective-permute-start | bytes 124424 | tf_op jit(solution)/shard_map/ppermute | solution.py:31
  74.8 3.6 %shard_map.92.summed_ref = f32[1296,256]{1,0:T(8,128)S(1)} custom-call(bf16[1536,512]{1,0:T(8,128)(2,1)S(1)} %get-tuple-element.67.inner_ref, bf16[512,512]{1,0:T(8,128)(2,1)S(1)} %get-tuple-element.70.outer_ref, s32[24,128]{1,0:T(8,128)S(1)} %scatter.15.index_ref), custom_call_target="tpu_custom_call" | custom-call | flops 2700000000 | bytes 3000000 | tf_op jit(solution)/shard_map/pallas_call | solution.py:184
  78.4 8.0 %collective-permute-done.3.back_ref = bf16[81,256]{1,0:T(8,128)(2,1)S(1)} collective-permute-done((bf16[81,256]{1,0:T(8,128)(2,1)S(1)}, bf16[81,256]{1,0:T(8,128)(2,1)S(1)}, u32[]{:S(2)}, u32[]{:S(2)}) %collective-permute-start.3) | collective-permute-done | bytes 41504 | tf_op jit(solution)/shard_map/ppermute | solution.py:31
  86.4 1.6 shard_map.93
  88.0 0.0 all-gather.2.cloned.1.call-update
  88.0 54.1 %all-gather.2.cloned.1.call-done = bf16[1296,2048]{1,0:T(8,128)(2,1)} async-done(((bf16[1296,256]{1,0:T(8,128)(2,1)}), bf16[1296,2048]{1,0:T(8,128)(2,1)}) %all-gather.2.cloned.1.call-update) | async-done | bytes 5308432 | tf_op jit(solution)/shard_map/all_gather | solution.py:294
  142.1 4.4 %convolution_convert_fusion = bf16[2048,256]{1,0:T(8,128)(2,1)S(1)} fusion(bf16[1296,2048]{1,0:T(8,128)(2,1)} %all-gather.2.cloned.1.call-done, bf16[1296,256]{1,0:T(8,128)(2,1)S(1)} %get-tuple-element.73), kind=kOutput, calls=%fused_computation.1 | convolution fusion | flops 1359478784 | bytes 7020544 | tf_op jit(solution)/shard_map/dot_general | solution.py:295
  146.5 56.5 %all_to_all.5 = bf16[128,16,256]{2,1,0:T(8,128)(2,1)S(1)} all-to-all(bf16[128,16,256]{2,1,0:T(8,128)(2,1)S(1)} %bitcast.6), channel_id=1, replica_groups=mesh['dom'=128,'band'=8] {'dom'}, dimensions={0} | all-to-all | bytes 2097152 | tf_op jit(solution)/shard_map/all_to_all | solution.py:299
  203.0 0.8 convert_reduce_fusion
  (1 shorter events, 0.0 us)
Async XLA Ops:
  7.2 134.9 %all-gather.2.cloned.1.call-start = ((), (), s32[]{:S(2)}) async-start(), calls=%async_computation.1 | async-start | bytes 5971968 | tf_op jit(solution)/shard_map/all_gather | solution.py:294
  9.7 36.2 %collective-permute-start = (bf16[81,256]{1,0:T(8,128)(2,1)S(1)}, bf16[81,256]{1,0:T(8,128)(2,1)S(1)}, u32[]{:S(2)}, u32[]{:S(2)}) collective-permute-start(bf16[81,256]{1,0:T(8,128)(2,1)S(1)} %gather_fusion), channel_id=1, source_target_pairs={{0,1016},{8,0},{16,8},{24,16},{32,24},{40,32},{48,40},{56,48},{64,... | collective-permute-start | bytes 124424 | tf_op jit(solution)/shard_map/ppermute | solution.py:31
  38.8 1.1 copy-start
  39.9 0.7 copy-start.2
  40.6 4.8 %copy-start.4 = (f32[1296]{0:T(1024)S(1)}, f32[1296]{0:T(1024)}, u32[]{:S(2)}) copy-start(f32[1296]{0:T(1024)} %param.20) | copy-start | bytes 15556
  40.6 5.1 %copy-start.5 = (f32[1296]{0:T(1024)S(1)}, f32[1296]{0:T(1024)}, u32[]{:S(2)}) copy-start(f32[1296]{0:T(1024)} %param.21) | copy-start | bytes 15556
  47.2 14.5 %collective-permute-start.1 = (bf16[81,256]{1,0:T(8,128)(2,1)S(1)}, bf16[81,256]{1,0:T(8,128)(2,1)S(1)}, u32[]{:S(2)}, u32[]{:S(2)}) collective-permute-start(bf16[81,256]{1,0:T(8,128)(2,1)S(1)} %get-tuple-element.65), channel_id=1, source_target_pairs={{0,8},{8,16},{16,24},{24,32},{32,40},{40,48},{48,56},{56,64},{64,7... | collective-permute-start | bytes 124424 | tf_op jit(solution)/shard_map/ppermute | solution.py:31
  49.1 12.6 %copy-start.1 = (bf16[1296,256]{1,0:T(8,128)(2,1)S(1)}, bf16[1296,256]{1,0:T(8,128)(2,1)}, u32[]{:S(2)}) copy-start(bf16[1296,256]{1,0:T(8,128)(2,1)} %values_ref.5) | copy-start | bytes 1990660
  52.8 12.9 %copy-start.3 = (f32[16]{0:T(128)S(1)}, f32[16]{0:T(128)}, u32[]{:S(2)}) copy-start(f32[16]{0:T(128)} %scale_ref.7) | copy-start | bytes 196
  62.6 8.0 %collective-permute-start.2 = (bf16[81,256]{1,0:T(8,128)(2,1)S(1)}, bf16[81,256]{1,0:T(8,128)(2,1)S(1)}, u32[]{:S(2)}, u32[]{:S(2)}) collective-permute-start(bf16[81,256]{1,0:T(8,128)(2,1)S(1)} %get-tuple-element.69), channel_id=1, source_target_pairs={{0,1016},{8,0},{16,8},{24,16},{32,24},{40,32},{48,40},{56,48},{64,... | collective-permute-start | bytes 124424 | tf_op jit(solution)/shard_map/ppermute | solution.py:31
  71.8 14.5 %collective-permute-start.3 = (bf16[81,256]{1,0:T(8,128)(2,1)S(1)}, bf16[81,256]{1,0:T(8,128)(2,1)S(1)}, u32[]{:S(2)}, u32[]{:S(2)}) collective-permute-start(bf16[81,256]{1,0:T(8,128)(2,1)S(1)} %get-tuple-element.71), channel_id=1, source_target_pairs={{0,8},{8,16},{16,24},{24,32},{32,40},{40,48},{48,56},{56,64},{64,7... | collective-permute-start | bytes 124424 | tf_op jit(solution)/shard_map/ppermute | solution.py:31
Sparse Core Ops, SparseCore 0:
  88.1 53.9 all-gather.1

commit v2 on v1

--- a/solution.py
+++ b/solution.py
@@ -4,6 +4,7 @@
 from jax.experimental import pallas as pl
 from jax.experimental.pallas import tpu as pltpu
 from jax.sharding import PartitionSpec as P
+
 
 filter_center = 5.0
 filter_width = 6.0
@@ -21,6 +22,8 @@
 OUTER_ENTRIES = ENTRIES - INNER_ENTRIES
 IFACE_SLOT = 16
 SLOTS = 24
+DOM = ("xh", "z", "y")
+CHIPS = 4
 BF = jnp.bfloat16
 F32 = jnp.float32
 
@@ -63,20 +66,58 @@
             out_ref[start : start + PAD, STATES_DEV:] = low
 
 
-def inner_kernel(scale_ref, values_ref, index_t_ref, element_ref, terms_ref, outer_ref, padded, match):
-    padded[:OWN, :] = values_ref[...]
-    padded[OWN:, :] = jnp.zeros((OWN_PAD - OWN, STATES_DEV), BF)
+def pick_entries(scale_ref, values, index_t_ref, element_ref, terms_ref, outer_ref, match):
     for group in range(4):
         for cell in range(4):
             number = group * 4 + cell
             match[cell * PAD : (cell + 1) * PAD, :] = rows_match(
                 index_t_ref[:, number : number + 1], OWN_PAD
             )
-        gathered = dot(match[...], padded[...]).astype(BF)
+        gathered = dot(match[...], values[...]).astype(BF)
         if group < 3:
             cell_products(gathered, element_ref, scale_ref, group * 4, terms_ref, group * 4 * PAD)
         else:
             outer_ref[...] = gathered
+
+
+def pad_values(padded, values):
+    padded[:OWN, :] = values
+    padded[OWN:, :] = jnp.zeros((OWN_PAD - OWN, STATES_DEV), BF)
+
+
+def first_kernel(
+    scale_ref,
+    values_ref,
+    cells_ref,
+    nodes_ref,
+    matrix_ref,
+    terms_ref,
+    outer_ref,
+    shared_ref,
+    index_ref,
+    index_t_ref,
+    element_ref,
+    padded,
+    match,
+    table,
+):
+    table[...] = jnp.full((PAD, PAD), -1, jnp.int32)
+    table[:CELLS, :NPC] = cells_ref[...]
+    table[IFACE_SLOT : IFACE_SLOT + 1, :SHARED] = nodes_ref[...]
+    index_ref[...] = table[:SLOTS, :]
+    index_t_ref[...] = jnp.transpose(table[...])
+    element_ref[...] = jnp.zeros_like(element_ref)
+    element_ref[:NPC, :NPC] = matrix_ref[...]
+    element_ref[PAD : PAD + NPC, PAD : PAD + NPC] = matrix_ref[...]
+    pad_values(padded, values_ref[...])
+    chosen = rows_match(index_t_ref[:, IFACE_SLOT : IFACE_SLOT + 1], OWN_PAD)
+    shared_ref[...] = dot(chosen, padded[...]).astype(BF)[:SHARED, :]
+    pick_entries(scale_ref, padded, index_t_ref, element_ref, terms_ref, outer_ref, match)
+
+
+def inner_kernel(scale_ref, values_ref, index_t_ref, element_ref, terms_ref, outer_ref, padded, match):
+    pad_values(padded, values_ref[...])
+    pick_entries(scale_ref, padded, index_t_ref, element_ref, terms_ref, outer_ref, match)
 
 
 def outer_kernel(
@@ -145,8 +186,7 @@
     own = (potential_ref[...] - filter_center) * (1.0 / filter_width)
     middle = (summed * factor + values_ref[...].astype(F32) * own).astype(BF)
     middle_ref[...] = middle
-    padded[:OWN, :] = middle
-    padded[OWN:, :] = jnp.zeros((OWN_PAD - OWN, STATES_DEV), BF)
+    pad_values(padded, middle)
     match = rows_match(index_t_ref[:, IFACE_SLOT : IFACE_SLOT + 1], OWN_PAD)
     shared_ref[...] = dot(match, padded[...]).astype(BF)[:SHARED, :]
 
@@ -196,20 +236,11 @@
     return jax.ShapeDtypeStruct((rows, columns), dtype)
 
 
-def summed_terms(values, shared, scales, index, index_t, element):
-    remote = shifted(shared, "dom", -1)
-    inner, outer = call(
-        inner_kernel,
-        1,
-        3,
-        [shape(INNER_ENTRIES, 2 * STATES_DEV, BF), shape(OUTER_ENTRIES, STATES_DEV, BF)],
-        [pltpu.VMEM((OWN_PAD, STATES_DEV), BF), pltpu.VMEM((4 * PAD, OWN_PAD), BF)],
-        1_600_000_000,
-        scales,
-        values,
-        index_t,
-        element,
-    )
+INNER_OUTS = [shape(INNER_ENTRIES, 2 * STATES_DEV, BF), shape(OUTER_ENTRIES, STATES_DEV, BF)]
+INNER_SCRATCH = [pltpu.VMEM((OWN_PAD, STATES_DEV), BF), pltpu.VMEM((4 * PAD, OWN_PAD), BF)]
+
+
+def summed_terms(inner, outer, remote, scales, index, index_t, element):
     outer_terms, back = call(
         outer_kernel,
         1,
@@ -224,7 +255,7 @@
         index_t,
         element,
     )
-    returned = shifted(back, "dom", 1)
+    returned = shifted(back, DOM, 1)
     (summed,) = call(
         spread_kernel,
         0,
@@ -242,17 +273,29 @@
 def filtered_states(
     filter_input, element_matrix, cell_scale, connectivity, interface_nodes, lumped_mass, potential
 ):
-    shared = filter_input[interface_nodes]
-    index = jnp.full((SLOTS, PAD), -1, jnp.int32)
-    index = index.at[:CELLS, :NPC].set(connectivity)
-    index = index.at[IFACE_SLOT, :SHARED].set(interface_nodes)
-    index_t = index.T
-    element = jnp.zeros((2 * PAD, 2 * PAD), BF)
-    element = element.at[:NPC, :NPC].set(element_matrix)
-    element = element.at[PAD : PAD + NPC, PAD : PAD + NPC].set(element_matrix)
+    inner, outer, shared, index, index_t, element = call(
+        first_kernel,
+        1,
+        4,
+        INNER_OUTS
+        + [
+            shape(SHARED, STATES_DEV, BF),
+            shape(SLOTS, PAD, jnp.int32),
+            shape(PAD, PAD, jnp.int32),
+            shape(2 * PAD, 2 * PAD, BF),
+        ],
+        INNER_SCRATCH + [pltpu.VMEM((PAD, PAD), jnp.int32)],
+        1_800_000_000,
+        cell_scale,
+        filter_input,
+        connectivity,
+        interface_nodes[None, :],
+        element_matrix,
+    )
     mass = lumped_mass[:, None]
     pot = potential[:, None]
-    summed, returned = summed_terms(filter_input, shared, cell_scale, index, index_t, element)
+    remote = shifted(shared, DOM, -1)
+    summed, returned = summed_terms(inner, outer, remote, cell_scale, index, index_t, element)
     middle, shared = call(
         middle_kernel,
         0,
@@ -268,8 +311,21 @@
         index,
         index_t,
     )
-    summed, returned = summed_terms(middle, shared, cell_scale, index, index_t, element)
-    node_total = OWN * lax.axis_size("dom")
+    remote = shifted(shared, DOM, -1)
+    inner, outer = call(
+        inner_kernel,
+        1,
+        3,
+        INNER_OUTS,
+        INNER_SCRATCH,
+        1_600_000_000,
+        cell_scale,
+        middle,
+        index_t,
+        element,
+    )
+    summed, returned = summed_terms(inner, outer, remote, cell_scale, index, index_t, element)
+    node_total = OWN * lax.axis_size(DOM)
     total = jnp.full((1,), 1.0 / float(node_total), F32)
     return call(
         final_kernel,
@@ -289,23 +345,99 @@
     )
 
 
+HELD = ((0, 1, 2, 3), (1, 2, 0, 3), (2, 1, 3, 0), (3, 2, 1, 0))
+
+
+def moved(value, axis, pairs):
+    return lax.ppermute(value, axis, pairs)
+
+
+def collect_kernel(place_ref, first_ref, second_ref, out_ref):
+    for number in range(8):
+        ref = first_ref if number < 4 else second_ref
+        terms = ref[:, number % 4].astype(F32)
+        out_ref[place_ref[number]] = jnp.sum(terms, axis=0).astype(BF)
+
+
+def block_terms(block, weights):
+    terms = lax.dot_general(
+        block, weights, (((0,), (0,)), ((), ())), preferred_element_type=jnp.float32
+    ).astype(BF)
+    return terms[:, :STATES_DEV], terms[:, STATES_DEV:]
+
+
+def by_line(pieces):
+    lines = lax.axis_size("y")
+    height = STATES_DEV * lax.axis_size("xl") * lax.axis_size("c") // lax.axis_size(DOM)
+    rows = [p.reshape(-1, lines, height, STATES_DEV) for p in pieces]
+    rows = jnp.concatenate(rows, axis=0)
+    rows = rows.reshape(len(pieces), -1, lines, height, STATES_DEV)
+    return rows.transpose(2, 0, 1, 3, 4)
+
+
+def over_y(sent):
+    return lax.all_to_all(sent, "y", 0, 0)
+
+
+def after(value, earlier):
+    return lax.optimization_barrier((value, earlier))[0]
+
+
+def intersection_tile(filtered, weighted):
+    chip = lax.axis_index("xl")
+    core = lax.axis_index("c")
+    swap = [(0, 1), (1, 0)]
+    right_1 = moved(filtered, "xl", [(0, 1), (1, 2), (2, 3)])
+    left_1 = moved(filtered, "xl", [(1, 0), (2, 1), (3, 2)])
+    weights = jnp.concatenate([weighted, moved(weighted, "c", swap)], axis=1)
+    mine_0, theirs_0 = block_terms(filtered, weights)
+    right_2 = moved(right_1, "xl", [(1, 2), (2, 3)])
+    left_2 = moved(left_1, "xl", [(1, 0), (2, 1)])
+    mine_1, theirs_1 = block_terms(jnp.where(chip < 2, left_1, right_1), weights)
+    swapped = moved(jnp.concatenate([theirs_0, theirs_1], axis=0), "c", swap)
+    sent = by_line([mine_0, swapped[:STATES_DEV], mine_1, swapped[STATES_DEV:]])
+    first = over_y(sent)
+    passed = jnp.where(chip == 1, left_2, right_2)
+    relayed = moved(passed, "xl", [(1, 0), (2, 3)])
+    slot_2 = jnp.where(
+        chip == 0, left_2, jnp.where(chip == 1, right_1, jnp.where(chip == 2, left_1, right_2))
+    )
+    mine_2, theirs_2 = block_terms(after(slot_2, sent), weights)
+    swapped_2 = moved(theirs_2, "c", swap)
+    slot_3 = jnp.where((chip == 1) | (chip == 2), passed, relayed)
+    mine_3, theirs_3 = block_terms(after(slot_3, sent), weights)
+    swapped_3 = moved(theirs_3, "c", swap)
+    second = over_y(by_line([mine_2, swapped_2, mine_3, swapped_3]))
+    blocks = jnp.asarray(HELD, jnp.int32)[chip]
+    place = jnp.stack([2 * blocks + core, 2 * blocks + 1 - core], axis=1).reshape(-1)
+    kept = pl.pallas_call(
+        collect_kernel,
+        out_shape=jax.ShapeDtypeStruct((8,) + first.shape[2:], BF),
+        in_specs=[SCALARS, ARRAY, ARRAY],
+        out_specs=ARRAY,
+        compiler_params=pltpu.CompilerParams(vmem_limit_bytes=LIMIT),
+    )(place.astype(jnp.int32), first, second)
+    planes = lax.axis_size(("xh", "z"))
+    pieces = lax.all_to_all(kept.reshape(planes, -1, STATES_DEV), ("xh", "z"), 0, 0)
+    return jnp.sum(pieces.astype(F32), axis=0)
+
+
 def per_device(*args):
     filtered, weighted = filtered_states(*args)
-    gathered = lax.all_gather(filtered, "band", axis=1, tiled=True)
-    terms = lax.dot_general(
-        gathered, weighted, (((0,), (0,)), ((), ())), preferred_element_type=jnp.float32
-    ).astype(BF)
-    domains = lax.axis_size("dom")
-    pieces = lax.all_to_all(terms.reshape(domains, -1, terms.shape[1]), "dom", 0, 0)
-    return filtered, jnp.sum(pieces.astype(F32), axis=0)
+    tile = intersection_tile(filtered, weighted)
+    return filtered, tile
 
 
 def solution(mesh):
-    placed = (P("dom", "band"), P(), P("dom"), P("dom", None), P("dom"), P("dom"), P("dom"))
+    fine = jax.sharding.Mesh(
+        mesh.devices.reshape(2, 8, 8, CHIPS, 2), ("xh", "z", "y", "xl", "c")
+    )
+    band = ("xl", "c")
+    placed = (P(DOM, band), P(), P(DOM), P(DOM, None), P(DOM), P(DOM), P(DOM))
     return jax.shard_map(
         per_device,
-        mesh=mesh,
+        mesh=fine,
         in_specs=placed,
-        out_specs=(P("dom", "band"), P("dom", "band")),
+        out_specs=(P(DOM, band), P(DOM, band)),
         check_vma=False,
     )

time: 211 us -> 173 us (0.82)
  blocking collectives: 56.5 us -> 15.5 us
  starting transfers between devices: 33 us -> 62.3 us
  waiting for transfers between devices: 71.1 us -> 55.6 us
  between operations: 14.2 us -> 1.08 us
  other arithmetic: 1.47 us -> 3.96 us
    all_gather x1 -> x0, waiting for transfers between devices: 54.1 us -> none  [per_device(): gathered = lax.all_gather(filtered, 'band', axis=1, tiled=True)]
    all_to_all x1, blocking collectives: 56.5 us -> 15.5 us  [intersection_tile(): lax.all_to_all(kept.reshape(planes, -1, STATES_DEV), ('xh', 'z'), 0, 0)]
    ppermute x0 -> x9, starting transfers between devices: none -> 22.4 us  [moved(): return lax.ppermute(value, axis, pairs)]
    all_to_all x0 -> x2, waiting for transfers between devices: none -> 18.4 us  [over_y(): return lax.all_to_all(sent, 'y', 0, 0)]
    ppermute x0 -> x9, waiting for transfers between devices: none -> 18.1 us  [moved(): return lax.ppermute(value, axis, pairs)]
    all_to_all x0 -> x2, starting transfers between devices: none -> 6.98 us  [over_y(): return lax.all_to_all(sent, 'y', 0, 0)]
    scatter x4 -> x0, local copies, waits for them, and re-layouts: 3.93 us -> none  [the longest x1 1.71 us: filtered_states(): element = element.at[PAD:PAD + NPC, PAD:PAD + NPC].set(element_matrix)]
    concatenate x0 -> x3, local copies, waits for them, and re-layouts: none -> 2.83 us  [the longest x2 1.7 us: by_line(): rows = jnp.concatenate(rows, axis=0)]
  transfers between devices with their start and end apart: 5 -> 15, of which waited for: 3 -> 10; matrix products, arithmetic and copies ran while one was open for 2% -> 5% of each run, Pallas kernels for 8% -> 7%
where the time goes in v2:
time: 173 us; the launch traced here: 172 us
  starting transfers between devices  62.3 us (36%)
  waiting for transfers between devices  55.6 us (32%)
  Pallas kernels  22.8 us (13%)
  blocking collectives  15.5 us (9%)
  local copies, waits for them, and re-layouts  7.93 us (5%)
  other arithmetic  3.96 us (2%)
  matrix products  2.36 us (1%)
    ppermute x4, starting transfers between devices, shifted(): return lax.ppermute(value, axis, pairs)  33 us
    ppermute x9, starting transfers between devices, moved(): return lax.ppermute(value, axis, pairs)  22.4 us
    pallas_call x8, Pallas kernels, call(): pl.pallas_call(body, out_shape=outs, in_specs=[SCALARS] * scalars + [ARRA...  22.1 us
    ppermute x4, waiting for transfers between devices, shifted(): return lax.ppermute(value, axis, pairs)  19 us
    all_to_all x2, waiting for transfers between devices, over_y(): return lax.all_to_all(sent, 'y', 0, 0)  18.4 us
    ppermute x9, waiting for transfers between devices, moved(): return lax.ppermute(value, axis, pairs)  18.1 us
    all_to_all x1, blocking collectives, intersection_tile(): lax.all_to_all(kept.reshape(planes, -1, STATES_DEV), ('xh', 'z'), 0, 0)  15.5 us
    all_to_all x2, starting transfers between devices, over_y(): return lax.all_to_all(sent, 'y', 0, 0)  6.98 us
  transfers between devices with their start and end apart: 15, of which 10 were waited for; matrix products, arithmetic and copies ran while one was open for 5% of the time, Pallas kernels for 7%

profile of v2, /device:TPU:2, one launch (start us, length us, event | category | flops | bytes accessed | tf_op | source)
XLA Modules:
  0.0 171.6 jit_solution(6006580902634864511)
XLA Ops:
  0.6 0.0 copy-start
  0.6 1.1 copy-done
  1.7 0.8 copy-done.2
  2.5 0.7 copy-done.3
  3.2 0.7 copy-done.4
  3.8 0.7 copy-done.5
  4.5 5.0 %shard_map.95 = (bf16[1536,512]{1,0:T(8,128)(2,1)S(1)}, bf16[512,256]{1,0:T(8,128)(2,1)S(1)}, bf16[81,256]{1,0:T(8,128)(2,1)S(1)}, s32[24,128]{1,0:T(8,128)S(1)}...) custom-call(f32[16]{0:T(128)S(1)} %copy-done.5, bf16[1296,256]{1,0:T(8,128)(2,1)S(1)} %copy-done, ...), custom_call_target="tpu_custom_call" | custom-call | flops 1800000000 | bytes 3000000 | tf_op jit(solution)/shard_map/pallas_call | solution.py:224
  9.5 25.0 %collective-permute-start = (bf16[81,256]{1,0:T(8,128)(2,1)S(1)}, bf16[81,256]{1,0:T(8,128)(2,1)S(1)}, u32[]{:S(2)}, u32[]{:S(2)}) collective-permute-start(bf16[81,256]{1,0:T(8,128)(2,1)S(1)} %get-tuple-element.22), channel_id=1, source_target_pairs={{0,1016},{8,0},{16,8},{24,16},{32,24},{40,32},{48,40},{56,48},{64,... | collective-permute-start | bytes 124424 | tf_op jit(solution)/shard_map/ppermute | solution.py:34
  34.5 0.2 broadcast_in_dim.12.mass_ref
  34.8 0.2 broadcast_in_dim.13.potential_ref
  35.0 1.6 collective-permute-done.remote_ref
  36.6 1.3 shard_map.96
  37.9 1.9 %collective-permute-start.1 = (bf16[81,256]{1,0:T(8,128)(2,1)S(1)}, bf16[81,256]{1,0:T(8,128)(2,1)S(1)}, u32[]{:S(2)}, u32[]{:S(2)}) collective-permute-start(bf16[81,256]{1,0:T(8,128)(2,1)S(1)} %get-tuple-element.27), channel_id=1, source_target_pairs={{0,8},{8,16},{16,24},{24,32},{32,40},{40,48},{48,56},{56,64},{64,7... | collective-permute-start | bytes 124424 | tf_op jit(solution)/shard_map/ppermute | solution.py:34
  39.8 0.0 copy-start.1
  39.8 3.6 %shard_map.97.summed_ref = f32[1296,256]{1,0:T(8,128)S(1)} custom-call(bf16[1536,512]{1,0:T(8,128)(2,1)S(1)} %get-tuple-element.20.inner_ref, bf16[512,512]{1,0:T(8,128)(2,1)S(1)} %get-tuple-element.26.outer_ref, s32[24,128]{1,0:T(8,128)S(1)} %get-tuple-element.23.index_ref), custom_call_target="tpu_custom_call" | custom-call | flops 2700000000 | bytes 3000000 | tf_op jit(solution)/shard_map/pallas_call | solution.py:224
  43.5 0.0 copy-start.6
  43.5 9.1 %collective-permute-done.1.back_ref = bf16[81,256]{1,0:T(8,128)(2,1)S(1)} collective-permute-done((bf16[81,256]{1,0:T(8,128)(2,1)S(1)}, bf16[81,256]{1,0:T(8,128)(2,1)S(1)}, u32[]{:S(2)}, u32[]{:S(2)}) %collective-permute-start.1) | collective-permute-done | bytes 41504 | tf_op jit(solution)/shard_map/ppermute | solution.py:34
  52.6 0.8 shard_map.98
  53.5 3.7 %collective-permute-start.2 = (bf16[81,256]{1,0:T(8,128)(2,1)S(1)}, bf16[81,256]{1,0:T(8,128)(2,1)S(1)}, u32[]{:S(2)}, u32[]{:S(2)}) collective-permute-start(bf16[81,256]{1,0:T(8,128)(2,1)S(1)} %get-tuple-element.31), channel_id=1, source_target_pairs={{0,1016},{8,0},{16,8},{24,16},{32,24},{40,32},{48,40},{56,48},{64,... | collective-permute-start | bytes 124424 | tf_op jit(solution)/shard_map/ppermute | solution.py:34
  57.2 4.8 %shard_map.99 = (bf16[1536,512]{1,0:T(8,128)(2,1)S(1)}, bf16[512,256]{1,0:T(8,128)(2,1)S(1)}) custom-call(f32[16]{0:T(128)S(1)} %copy-done.6, bf16[1296,256]{1,0:T(8,128)(2,1)S(1)} %get-tuple-element.28.values_ref.middle_ref, s32[128,128]{1,0:T(8,128)S(1)} %get-tuple-element.24.index_t_ref, bf16[256,256]{1,0:T(8,128)(2,1)S(1)} %get-tuple-element.25.element_ref), custom_call_target="tpu_custom_call" | custom-call | flops 1600000000 | bytes 3000000 | tf_op jit(solution)/shard_map/pallas_call | solution.py:224
  62.0 0.0 collective-permute-done.2.remote_ref
  62.0 1.3 shard_map.100
  63.3 2.3 %collective-permute-start.3 = (bf16[81,256]{1,0:T(8,128)(2,1)S(1)}, bf16[81,256]{1,0:T(8,128)(2,1)S(1)}, u32[]{:S(2)}, u32[]{:S(2)}) collective-permute-start(bf16[81,256]{1,0:T(8,128)(2,1)S(1)} %get-tuple-element.33), channel_id=1, source_target_pairs={{0,8},{8,16},{16,24},{24,32},{32,40},{40,48},{48,56},{56,64},{64,7... | collective-permute-start | bytes 124424 | tf_op jit(solution)/shard_map/ppermute | solution.py:34
  65.7 3.6 %shard_map.101.summed_ref = f32[1296,256]{1,0:T(8,128)S(1)} custom-call(bf16[1536,512]{1,0:T(8,128)(2,1)S(1)} %get-tuple-element.29.inner_ref, bf16[512,512]{1,0:T(8,128)(2,1)S(1)} %get-tuple-element.32.outer_ref, s32[24,128]{1,0:T(8,128)S(1)} %get-tuple-element.23.index_ref), custom_call_target="tpu_custom_call" | custom-call | flops 2700000000 | bytes 3000000 | tf_op jit(solution)/shard_map/pallas_call | solution.py:224
  69.3 8.3 %collective-permute-done.3.back_ref = bf16[81,256]{1,0:T(8,128)(2,1)S(1)} collective-permute-done((bf16[81,256]{1,0:T(8,128)(2,1)S(1)}, bf16[81,256]{1,0:T(8,128)(2,1)S(1)}, u32[]{:S(2)}, u32[]{:S(2)}) %collective-permute-start.3) | collective-permute-done | bytes 41504 | tf_op jit(solution)/shard_map/ppermute | solution.py:34
  77.6 1.7 shard_map.102
  79.3 2.1 %collective-permute-start.6 = (bf16[1296,256]{1,0:T(8,128)(2,1)}, bf16[1296,256]{1,0:T(8,128)(2,1)S(1)}, u32[]{:S(2)}, u32[]{:S(2)}) collective-permute-start(bf16[1296,256]{1,0:T(8,128)(2,1)} %get-tuple-element.18), channel_id=1, source_target_pairs={{0,2},{2,4},{4,6},{1,3},{3,5},{5,7},{8,10},{10,12},{12,14},{9,11},... | collective-permute-start | bytes 1990664 | tf_op jit(solution)/shard_map/ppermute | solution.py:352
  81.3 3.8 %collective-permute-start.5 = (bf16[1296,256]{1,0:T(8,128)(2,1)}, bf16[1296,256]{1,0:T(8,128)(2,1)S(1)}, u32[]{:S(2)}, u32[]{:S(2)}) collective-permute-start(bf16[1296,256]{1,0:T(8,128)(2,1)} %get-tuple-element.18), channel_id=1, source_target_pairs={{2,0},{4,2},{6,4},{3,1},{5,3},{7,5},{10,8},{12,10},{14,12},{11,9},... | collective-permute-start | bytes 1990664 | tf_op jit(solution)/shard_map/ppermute | solution.py:352
  85.2 1.9 %collective-permute-start.4 = (bf16[1296,256]{1,0:T(8,128)(2,1)S(1)}, bf16[1296,256]{1,0:T(8,128)(2,1)}, u32[]{:S(2)}, u32[]{:S(2)}) collective-permute-start(bf16[1296,256]{1,0:T(8,128)(2,1)S(1)} %get-tuple-element.35), channel_id=1, source_target_pairs={{0,1},{1,0},{2,3},{3,2},{4,5},{5,4},{6,7},{7,6},{8,9},{9,8},{10,11... | collective-permute-start | bytes 1990664 | tf_op jit(solution)/shard_map/ppermute | solution.py:352
  87.2 7.9 %collective-permute-done.6 = bf16[1296,256]{1,0:T(8,128)(2,1)S(1)} collective-permute-done((bf16[1296,256]{1,0:T(8,128)(2,1)}, bf16[1296,256]{1,0:T(8,128)(2,1)S(1)}, u32[]{:S(2)}, u32[]{:S(2)}) %collective-permute-start.6) | collective-permute-done | bytes 663584 | tf_op jit(solution)/shard_map/ppermute | solution.py:352
  95.1 2.2 %collective-permute-start.9 = (bf16[1296,256]{1,0:T(8,128)(2,1)S(1)}, bf16[1296,256]{1,0:T(8,128)(2,1)S(1)}, u32[]{:S(2)}, u32[]{:S(2)}) collective-permute-start(bf16[1296,256]{1,0:T(8,128)(2,1)S(1)} %collective-permute-done.6), channel_id=1, source_target_pairs={{2,4},{4,6},{3,5},{5,7},{10,12},{12,14},{11,13},{13,15},{18,20},{2... | collective-permute-start | bytes 1990664 | tf_op jit(solution)/shard_map/ppermute | solution.py:352
  97.3 0.0 collective-permute-done.5
  97.3 3.4 %collective-permute-start.8 = (bf16[1296,256]{1,0:T(8,128)(2,1)S(1)}, bf16[1296,256]{1,0:T(8,128)(2,1)S(1)}, u32[]{:S(2)}, u32[]{:S(2)}) collective-permute-start(bf16[1296,256]{1,0:T(8,128)(2,1)S(1)} %collective-permute-done.5), channel_id=1, source_target_pairs={{2,0},{4,2},{3,1},{5,3},{10,8},{12,10},{11,9},{13,11},{18,16},{20,... | collective-permute-start | bytes 1990664 | tf_op jit(solution)/shard_map/ppermute | solution.py:352
  100.7 1.1 constant_dynamic-update-slice_fusion
  101.8 0.0 copy-start.10
  101.8 0.6 convolution_convert_fusion.2
  102.5 0.4 copy-done.10
  102.9 0.6 convolution_convert_fusion.3
  103.6 1.9 %collective-permute-start.7 = (bf16[512,256]{1,0:T(8,128)(2,1)S(1)}, bf16[512,256]{1,0:T(8,128)(2,1)S(1)}, u32[]{:S(2)}, u32[]{:S(2)}) collective-permute-start(bf16[512,256]{1,0:T(8,128)(2,1)S(1)} %pad_maximum_fusion.2), channel_id=1, source_target_pairs={{0,1},{1,0},{2,3},{3,2},{4,5},{5,4},{6,7},{7,6},{8,9},{9,8},{10,11... | collective-permute-start | bytes 786440 | tf_op jit(solution)/shard_map/ppermute | solution.py:352
  105.5 2.2 %collective-permute-done.9 = bf16[1296,256]{1,0:T(8,128)(2,1)S(1)} collective-permute-done((bf16[1296,256]{1,0:T(8,128)(2,1)S(1)}, bf16[1296,256]{1,0:T(8,128)(2,1)S(1)}, u32[]{:S(2)}, u32[]{:S(2)}) %collective-permute-start.9) | collective-permute-done | bytes 663584 | tf_op jit(solution)/shard_map/ppermute | solution.py:352
  107.7 4.2 %collective-permute-done.8 = bf16[1296,256]{1,0:T(8,128)(2,1)S(1)} collective-permute-done((bf16[1296,256]{1,0:T(8,128)(2,1)S(1)}, bf16[1296,256]{1,0:T(8,128)(2,1)S(1)}, u32[]{:S(2)}, u32[]{:S(2)}) %collective-permute-start.8) | collective-permute-done | bytes 663584 | tf_op jit(solution)/shard_map/ppermute | solution.py:352
  111.9 1.3 select_select_fusion
  113.2 3.2 %collective-permute-start.11 = (bf16[1296,256]{1,0:T(8,128)(2,1)}, bf16[1296,256]{1,0:T(8,128)(2,1)S(1)}, u32[]{:S(2)}, u32[]{:S(2)}) collective-permute-start(bf16[1296,256]{1,0:T(8,128)(2,1)} %get-tuple-element.39), channel_id=1, source_target_pairs={{2,0},{4,6},{3,1},{5,7},{10,8},{12,14},{11,9},{13,15},{18,16},{20,... | collective-permute-start | bytes 1990664 | tf_op jit(solution)/shard_map/ppermute | solution.py:352
  116.5 0.1 pad_maximum_fusion
  116.6 0.8 copy.32
  117.4 3.5 %all-to-all-start = ((bf16[8,4,2,16,256]{4,3,2,1,0:T(8,128)(2,1)}), bf16[8,4,2,16,256]{4,3,2,1,0:T(8,128)(2,1)S(1)}, u32[]{:S(2)}, u32[]{:S(2)}) async-start(bf16[8,4,2,16,256]{4,3,2,1,0:T(8,128)(2,1)} %bitcast.8), calls=%async_computation | async-start | bytes 1048576 | tf_op jit(solution)/shard_map/all_to_all | solution.py:379
  120.9 0.6 convolution_convert_fusion.1
  121.6 1.9 %collective-permute-start.10 = (bf16[256,256]{1,0:T(8,128)(2,1)S(1)}, bf16[256,256]{1,0:T(8,128)(2,1)S(1)}, u32[]{:S(2)}, u32[]{:S(2)}) collective-permute-start(bf16[256,256]{1,0:T(8,128)(2,1)S(1)} %get-tuple-element.41), channel_id=1, source_target_pairs={{0,1},{1,0},{2,3},{3,2},{4,5},{5,4},{6,7},{7,6},{8,9},{9,8},{10,11... | collective-permute-start | bytes 393224 | tf_op jit(solution)/shard_map/ppermute | solution.py:352
  123.5 2.5 %collective-permute-done.11 = bf16[1296,256]{1,0:T(8,128)(2,1)S(1)} collective-permute-done((bf16[1296,256]{1,0:T(8,128)(2,1)}, bf16[1296,256]{1,0:T(8,128)(2,1)S(1)}, u32[]{:S(2)}, u32[]{:S(2)}) %collective-permute-start.11) | collective-permute-done | bytes 663584 | tf_op jit(solution)/shard_map/ppermute | solution.py:352
  126.0 1.2 broadcast_select_fusion
  127.1 0.6 convolution_convert_fusion
  127.7 1.9 %collective-permute-start.12 = (bf16[256,256]{1,0:T(8,128)(2,1)S(1)}, bf16[256,256]{1,0:T(8,128)(2,1)S(1)}, u32[]{:S(2)}, u32[]{:S(2)}) collective-permute-start(bf16[256,256]{1,0:T(8,128)(2,1)S(1)} %get-tuple-element.43), channel_id=1, source_target_pairs={{0,1},{1,0},{2,3},{3,2},{4,5},{5,4},{6,7},{7,6},{8,9},{9,8},{10,11... | collective-permute-start | bytes 393224 | tf_op jit(solution)/shard_map/ppermute | solution.py:352
  129.7 1.3 collective-permute-done.12
  131.0 0.1 pad_maximum_fusion.1
  131.1 0.9 copy.33
  131.9 2.2 %all-to-all-done.first_ref = bf16[8,4,2,16,256]{4,3,2,1,0:T(8,128)(2,1)S(1)} async-done(((bf16[8,4,2,16,256]{4,3,2,1,0:T(8,128)(2,1)}), bf16[8,4,2,16,256]{4,3,2,1,0:T(8,128)(2,1)S(1)}, u32[]{:S(2)}, u32[]{:S(2)}) %all-to-all-start) | async-done | bytes 524320 | tf_op jit(solution)/shard_map/all_to_all | solution.py:379
  134.1 3.5 %all-to-all-start.1 = ((bf16[8,4,2,16,256]{4,3,2,1,0:T(8,128)(2,1)}), bf16[8,4,2,16,256]{4,3,2,1,0:T(8,128)(2,1)S(1)}, u32[]{:S(2)}, u32[]{:S(2)}) async-start(bf16[8,4,2,16,256]{4,3,2,1,0:T(8,128)(2,1)} %bitcast.15), calls=%async_computation.1 | async-start | bytes 1048576 | tf_op jit(solution)/shard_map/all_to_all | solution.py:379
  137.6 0.7 add_bitcast_fusion
  138.4 0.1 copy.23
  138.5 0.1 reshape.71.place_ref
  138.5 16.2 %all-to-all-done.1.second_ref = bf16[8,4,2,16,256]{4,3,2,1,0:T(8,128)(2,1)S(1)} async-done(((bf16[8,4,2,16,256]{4,3,2,1,0:T(8,128)(2,1)}), bf16[8,4,2,16,256]{4,3,2,1,0:T(8,128)(2,1)S(1)}, u32[]{:S(2)}, u32[]{:S(2)}) %all-to-all-start.1) | async-done | bytes 524320 | tf_op jit(solution)/shard_map/all_to_all | solution.py:379
  154.7 0.7 shard_map.103
  155.4 15.5 %all_to_all.15 = bf16[16,16,256]{2,1,0:T(8,128)(2,1)S(1)} all-to-all(bf16[16,16,256]{2,1,0:T(8,128)(2,1)S(1)} %bitcast.27), channel_id=1, replica_groups=mesh['xh'=2,'z'=8,'y'=8,'xl'=4,'c'=2] {'xh','z'}, dimensions={0} | all-to-all | bytes 262144 | tf_op jit(solution)/shard_map/all_to_all | solution.py:421
  171.0 0.6 convert_reduce_fusion
  (23 shorter events, 0.2 us)
Async XLA Ops:
  0.6 1.1 copy-start
  1.7 0.8 copy-start.2
  2.5 0.7 copy-start.3
  3.2 0.7 copy-start.4
  3.8 0.7 copy-start.5
  4.5 30.0 %copy-start.8 = (f32[1296]{0:T(1024)S(1)}, f32[1296]{0:T(1024)}, u32[]{:S(2)}) copy-start(f32[1296]{0:T(1024)} %param.13) | copy-start | bytes 15556
  4.5 30.3 %copy-start.9 = (f32[1296]{0:T(1024)S(1)}, f32[1296]{0:T(1024)}, u32[]{:S(2)}) copy-start(f32[1296]{0:T(1024)} %param.14) | copy-start | bytes 15556
  9.5 27.1 %collective-permute-start = (bf16[81,256]{1,0:T(8,128)(2,1)S(1)}, bf16[81,256]{1,0:T(8,128)(2,1)S(1)}, u32[]{:S(2)}, u32[]{:S(2)}) collective-permute-start(bf16[81,256]{1,0:T(8,128)(2,1)S(1)} %get-tuple-element.22), channel_id=1, source_target_pairs={{0,1016},{8,0},{16,8},{24,16},{32,24},{40,32},{48,40},{56,48},{64,... | collective-permute-start | bytes 124424 | tf_op jit(solution)/shard_map/ppermute | solution.py:34
  37.9 14.7 %collective-permute-start.1 = (bf16[81,256]{1,0:T(8,128)(2,1)S(1)}, bf16[81,256]{1,0:T(8,128)(2,1)S(1)}, u32[]{:S(2)}, u32[]{:S(2)}) collective-permute-start(bf16[81,256]{1,0:T(8,128)(2,1)S(1)} %get-tuple-element.27), channel_id=1, source_target_pairs={{0,8},{8,16},{16,24},{24,32},{32,40},{40,48},{48,56},{56,64},{64,7... | collective-permute-start | bytes 124424 | tf_op jit(solution)/shard_map/ppermute | solution.py:34
  39.8 12.8 %copy-start.1 = (bf16[1296,256]{1,0:T(8,128)(2,1)S(1)}, bf16[1296,256]{1,0:T(8,128)(2,1)}, u32[]{:S(2)}) copy-start(bf16[1296,256]{1,0:T(8,128)(2,1)} %values_ref.5) | copy-start | bytes 1990660
  43.5 13.7 %copy-start.6 = (f32[16]{0:T(128)S(1)}, f32[16]{0:T(128)}, u32[]{:S(2)}) copy-start(f32[16]{0:T(128)} %scale_ref.7) | copy-start | bytes 196
  53.5 8.6 %collective-permute-start.2 = (bf16[81,256]{1,0:T(8,128)(2,1)S(1)}, bf16[81,256]{1,0:T(8,128)(2,1)S(1)}, u32[]{:S(2)}, u32[]{:S(2)}) collective-permute-start(bf16[81,256]{1,0:T(8,128)(2,1)S(1)} %get-tuple-element.31), channel_id=1, source_target_pairs={{0,1016},{8,0},{16,8},{24,16},{32,24},{40,32},{48,40},{56,48},{64,... | collective-permute-start | bytes 124424 | tf_op jit(solution)/shard_map/ppermute | solution.py:34
  63.3 14.3 %collective-permute-start.3 = (bf16[81,256]{1,0:T(8,128)(2,1)S(1)}, bf16[81,256]{1,0:T(8,128)(2,1)S(1)}, u32[]{:S(2)}, u32[]{:S(2)}) collective-permute-start(bf16[81,256]{1,0:T(8,128)(2,1)S(1)} %get-tuple-element.33), channel_id=1, source_target_pairs={{0,8},{8,16},{16,24},{24,32},{32,40},{40,48},{48,56},{56,64},{64,7... | collective-permute-start | bytes 124424 | tf_op jit(solution)/shard_map/ppermute | solution.py:34
  79.3 15.8 %collective-permute-start.6 = (bf16[1296,256]{1,0:T(8,128)(2,1)}, bf16[1296,256]{1,0:T(8,128)(2,1)S(1)}, u32[]{:S(2)}, u32[]{:S(2)}) collective-permute-start(bf16[1296,256]{1,0:T(8,128)(2,1)} %get-tuple-element.18), channel_id=1, source_target_pairs={{0,2},{2,4},{4,6},{1,3},{3,5},{5,7},{8,10},{10,12},{12,14},{9,11},... | collective-permute-start | bytes 1990664 | tf_op jit(solution)/shard_map/ppermute | solution.py:352
  81.3 16.0 %collective-permute-start.5 = (bf16[1296,256]{1,0:T(8,128)(2,1)}, bf16[1296,256]{1,0:T(8,128)(2,1)S(1)}, u32[]{:S(2)}, u32[]{:S(2)}) collective-permute-start(bf16[1296,256]{1,0:T(8,128)(2,1)} %get-tuple-element.18), channel_id=1, source_target_pairs={{2,0},{4,2},{6,4},{3,1},{5,3},{7,5},{10,8},{12,10},{14,12},{11,9},... | collective-permute-start | bytes 1990664 | tf_op jit(solution)/shard_map/ppermute | solution.py:352
  85.2 15.5 %collective-permute-start.4 = (bf16[1296,256]{1,0:T(8,128)(2,1)S(1)}, bf16[1296,256]{1,0:T(8,128)(2,1)}, u32[]{:S(2)}, u32[]{:S(2)}) collective-permute-start(bf16[1296,256]{1,0:T(8,128)(2,1)S(1)} %get-tuple-element.35), channel_id=1, source_target_pairs={{0,1},{1,0},{2,3},{3,2},{4,5},{5,4},{6,7},{7,6},{8,9},{9,8},{10,11... | collective-permute-start | bytes 1990664 | tf_op jit(solution)/shard_map/ppermute | solution.py:352
  95.1 12.7 %collective-permute-start.9 = (bf16[1296,256]{1,0:T(8,128)(2,1)S(1)}, bf16[1296,256]{1,0:T(8,128)(2,1)S(1)}, u32[]{:S(2)}, u32[]{:S(2)}) collective-permute-start(bf16[1296,256]{1,0:T(8,128)(2,1)S(1)} %collective-permute-done.6), channel_id=1, source_target_pairs={{2,4},{4,6},{3,5},{5,7},{10,12},{12,14},{11,13},{13,15},{18,20},{2... | collective-permute-start | bytes 1990664 | tf_op jit(solution)/shard_map/ppermute | solution.py:352
  97.3 14.6 %collective-permute-start.8 = (bf16[1296,256]{1,0:T(8,128)(2,1)S(1)}, bf16[1296,256]{1,0:T(8,128)(2,1)S(1)}, u32[]{:S(2)}, u32[]{:S(2)}) collective-permute-start(bf16[1296,256]{1,0:T(8,128)(2,1)S(1)} %collective-permute-done.5), channel_id=1, source_target_pairs={{2,0},{4,2},{3,1},{5,3},{10,8},{12,10},{11,9},{13,11},{18,16},{20,... | collective-permute-start | bytes 1990664 | tf_op jit(solution)/shard_map/ppermute | solution.py:352
  101.8 1.1 copy-start.10
  103.6 12.9 %collective-permute-start.7 = (bf16[512,256]{1,0:T(8,128)(2,1)S(1)}, bf16[512,256]{1,0:T(8,128)(2,1)S(1)}, u32[]{:S(2)}, u32[]{:S(2)}) collective-permute-start(bf16[512,256]{1,0:T(8,128)(2,1)S(1)} %pad_maximum_fusion.2), channel_id=1, source_target_pairs={{0,1},{1,0},{2,3},{3,2},{4,5},{5,4},{6,7},{7,6},{8,9},{9,8},{10,11... | collective-permute-start | bytes 786440 | tf_op jit(solution)/shard_map/ppermute | solution.py:352
  113.2 12.7 %collective-permute-start.11 = (bf16[1296,256]{1,0:T(8,128)(2,1)}, bf16[1296,256]{1,0:T(8,128)(2,1)S(1)}, u32[]{:S(2)}, u32[]{:S(2)}) collective-permute-start(bf16[1296,256]{1,0:T(8,128)(2,1)} %get-tuple-element.39), channel_id=1, source_target_pairs={{2,0},{4,6},{3,1},{5,7},{10,8},{12,14},{11,9},{13,15},{18,16},{20,... | collective-permute-start | bytes 1990664 | tf_op jit(solution)/shard_map/ppermute | solution.py:352
  116.5 4.4 %copy-start.7 = (bf16[1296,256]{1,0:T(8,128)(2,1)S(1)}, bf16[1296,256]{1,0:T(8,128)(2,1)}, u32[]{:S(2)}) copy-start(bf16[1296,256]{1,0:T(8,128)(2,1)} %get-tuple-element.36) | copy-start | bytes 1990660
  117.4 16.7 %all-to-all-start = ((bf16[8,4,2,16,256]{4,3,2,1,0:T(8,128)(2,1)}), bf16[8,4,2,16,256]{4,3,2,1,0:T(8,128)(2,1)S(1)}, u32[]{:S(2)}, u32[]{:S(2)}) async-start(bf16[8,4,2,16,256]{4,3,2,1,0:T(8,128)(2,1)} %bitcast.8), calls=%async_computation | async-start | bytes 1048576 | tf_op jit(solution)/shard_map/all_to_all | solution.py:379
  121.6 8.1 %collective-permute-start.10 = (bf16[256,256]{1,0:T(8,128)(2,1)S(1)}, bf16[256,256]{1,0:T(8,128)(2,1)S(1)}, u32[]{:S(2)}, u32[]{:S(2)}) collective-permute-start(bf16[256,256]{1,0:T(8,128)(2,1)S(1)} %get-tuple-element.41), channel_id=1, source_target_pairs={{0,1},{1,0},{2,3},{3,2},{4,5},{5,4},{6,7},{7,6},{8,9},{9,8},{10,11... | collective-permute-start | bytes 393224 | tf_op jit(solution)/shard_map/ppermute | solution.py:352
  127.7 3.2 %collective-permute-start.12 = (bf16[256,256]{1,0:T(8,128)(2,1)S(1)}, bf16[256,256]{1,0:T(8,128)(2,1)S(1)}, u32[]{:S(2)}, u32[]{:S(2)}) collective-permute-start(bf16[256,256]{1,0:T(8,128)(2,1)S(1)} %get-tuple-element.43), channel_id=1, source_target_pairs={{0,1},{1,0},{2,3},{3,2},{4,5},{5,4},{6,7},{7,6},{8,9},{9,8},{10,11... | collective-permute-start | bytes 393224 | tf_op jit(solution)/shard_map/ppermute | solution.py:352
  134.1 20.6 %all-to-all-start.1 = ((bf16[8,4,2,16,256]{4,3,2,1,0:T(8,128)(2,1)}), bf16[8,4,2,16,256]{4,3,2,1,0:T(8,128)(2,1)S(1)}, u32[]{:S(2)}, u32[]{:S(2)}) async-start(bf16[8,4,2,16,256]{4,3,2,1,0:T(8,128)(2,1)} %bitcast.15), calls=%async_computation.1 | async-start | bytes 1048576 | tf_op jit(solution)/shard_map/all_to_all | solution.py:379

commit v3 on v2

--- a/solution.py
+++ b/solution.py
@@ -352,10 +352,12 @@
     return lax.ppermute(value, axis, pairs)
 
 
-def collect_kernel(place_ref, first_ref, second_ref, out_ref):
-    for number in range(8):
-        ref = first_ref if number < 4 else second_ref
-        terms = ref[:, number % 4].astype(F32)
+def collect_kernel(place_ref, first_ref, second_ref, third_ref, out_ref):
+    pieces = [(first_ref, piece) for piece in range(4)]
+    pieces += [(second_ref, piece) for piece in range(2)]
+    pieces += [(third_ref, piece) for piece in range(2)]
+    for number, (ref, piece) in enumerate(pieces):
+        terms = ref[:, piece].astype(F32)
         out_ref[place_ref[number]] = jnp.sum(terms, axis=0).astype(BF)
 
 
@@ -389,7 +391,8 @@
     swap = [(0, 1), (1, 0)]
     right_1 = moved(filtered, "xl", [(0, 1), (1, 2), (2, 3)])
     left_1 = moved(filtered, "xl", [(1, 0), (2, 1), (3, 2)])
-    weights = jnp.concatenate([weighted, moved(weighted, "c", swap)], axis=1)
+    other = moved(weighted, "c", swap)
+    weights = jnp.concatenate([weighted, other], axis=1)
     mine_0, theirs_0 = block_terms(filtered, weights)
     right_2 = moved(right_1, "xl", [(1, 2), (2, 3)])
     left_2 = moved(left_1, "xl", [(1, 0), (2, 1)])
@@ -399,24 +402,27 @@
     first = over_y(sent)
     passed = jnp.where(chip == 1, left_2, right_2)
     relayed = moved(passed, "xl", [(1, 0), (2, 3)])
+    left_2, right_2, passed = lax.optimization_barrier((left_2, right_2, passed))
     slot_2 = jnp.where(
         chip == 0, left_2, jnp.where(chip == 1, right_1, jnp.where(chip == 2, left_1, right_2))
     )
     mine_2, theirs_2 = block_terms(after(slot_2, sent), weights)
-    swapped_2 = moved(theirs_2, "c", swap)
+    swapped = moved(theirs_2, "c", swap)
+    sent = by_line([mine_2, swapped])
+    second = over_y(sent)
     slot_3 = jnp.where((chip == 1) | (chip == 2), passed, relayed)
     mine_3, theirs_3 = block_terms(after(slot_3, sent), weights)
-    swapped_3 = moved(theirs_3, "c", swap)
-    second = over_y(by_line([mine_2, swapped_2, mine_3, swapped_3]))
+    swapped = moved(theirs_3, "c", swap)
+    third = over_y(by_line([mine_3, swapped]))
     blocks = jnp.asarray(HELD, jnp.int32)[chip]
     place = jnp.stack([2 * blocks + core, 2 * blocks + 1 - core], axis=1).reshape(-1)
     kept = pl.pallas_call(
         collect_kernel,
         out_shape=jax.ShapeDtypeStruct((8,) + first.shape[2:], BF),
-        in_specs=[SCALARS, ARRAY, ARRAY],
+        in_specs=[SCALARS, ARRAY, ARRAY, ARRAY],
         out_specs=ARRAY,
         compiler_params=pltpu.CompilerParams(vmem_limit_bytes=LIMIT),
-    )(place.astype(jnp.int32), first, second)
+    )(place.astype(jnp.int32), first, second, third)
     planes = lax.axis_size(("xh", "z"))
     pieces = lax.all_to_all(kept.reshape(planes, -1, STATES_DEV), ("xh", "z"), 0, 0)
     return jnp.sum(pieces.astype(F32), axis=0)

time: 173 us -> 204 us (1.18)
  waiting for transfers between devices: 55.6 us -> 79.7 us
  other arithmetic: 3.96 us -> 6.44 us
    ppermute x9, waiting for transfers between devices: 18.1 us -> 30.5 us  [moved(): return lax.ppermute(value, axis, pairs)]
    all_to_all x2 -> x3, waiting for transfers between devices: 18.4 us -> 30.2 us  [over_y(): return lax.all_to_all(sent, 'y', 0, 0)]
    all_to_all x2 -> x3, starting transfers between devices: 6.98 us -> 10.3 us  [over_y(): return lax.all_to_all(sent, 'y', 0, 0)]
    ppermute x9, starting transfers between devices: 22.4 us -> 20.2 us  [moved(): return lax.ppermute(value, axis, pairs)]
    unnamed x23 -> x21, local copies, waits for them, and re-layouts: 4.37 us -> 3.92 us
  transfers between devices with their start and end apart: 15 -> 16, of which waited for: 10 -> 13; matrix products, arithmetic and copies ran while one was open for 5% -> 5% of each run, Pallas kernels for 7% -> 6%
where the time goes in v3:
time: 204 us; the launch traced here: 203 us
  waiting for transfers between devices  79.7 us (39%)
  starting transfers between devices  63.5 us (31%)
  Pallas kernels  22.8 us (11%)
  blocking collectives  17 us (8%)
  local copies, waits for them, and re-layouts  9.72 us (5%)
  other arithmetic  6.44 us (3%)
  matrix products  2.36 us (1%)
    ppermute x4, starting transfers between devices, shifted(): return lax.ppermute(value, axis, pairs)  33 us
    ppermute x9, waiting for transfers between devices, moved(): return lax.ppermute(value, axis, pairs)  30.5 us
    all_to_all x3, waiting for transfers between devices, over_y(): return lax.all_to_all(sent, 'y', 0, 0)  30.2 us
    pallas_call x8, Pallas kernels, call(): pl.pallas_call(body, out_shape=outs, in_specs=[SCALARS] * scalars + [ARRA...  22.2 us
    ppermute x9, starting transfers between devices, moved(): return lax.ppermute(value, axis, pairs)  20.2 us
    ppermute x4, waiting for transfers between devices, shifted(): return lax.ppermute(value, axis, pairs)  19 us
    all_to_all x1, blocking collectives, intersection_tile(): lax.all_to_all(kept.reshape(planes, -1, STATES_DEV), ('xh', 'z'), 0, 0)  17 us
    all_to_all x3, starting transfers between devices, over_y(): return lax.all_to_all(sent, 'y', 0, 0)  10.3 us
  transfers between devices with their start and end apart: 16, of which 13 were waited for; matrix products, arithmetic and copies ran while one was open for 5% of the time, Pallas kernels for 6%

profile of v3, /device:TPU:2, one launch (start us, length us, event | category | flops | bytes accessed | tf_op | source)
XLA Modules:
  0.0 202.7 jit_solution(868685847694899677)
XLA Ops:
  0.6 1.1 copy-done
  1.7 0.8 copy-done.2
  2.5 0.7 copy-done.3
  3.2 0.7 copy-done.4
  3.8 0.7 copy-done.5
  4.5 5.0 %shard_map.95 = (bf16[1536,512]{1,0:T(8,128)(2,1)S(1)}, bf16[512,256]{1,0:T(8,128)(2,1)S(1)}, bf16[81,256]{1,0:T(8,128)(2,1)S(1)}, s32[24,128]{1,0:T(8,128)S(1)}...) custom-call(f32[16]{0:T(128)S(1)} %copy-done.5, bf16[1296,256]{1,0:T(8,128)(2,1)S(1)} %copy-done, ...), custom_call_target="tpu_custom_call" | custom-call | flops 1800000000 | bytes 3000000 | tf_op jit(solution)/shard_map/pallas_call | solution.py:224
  9.5 25.0 %collective-permute-start = (bf16[81,256]{1,0:T(8,128)(2,1)S(1)}, bf16[81,256]{1,0:T(8,128)(2,1)S(1)}, u32[]{:S(2)}, u32[]{:S(2)}) collective-permute-start(bf16[81,256]{1,0:T(8,128)(2,1)S(1)} %get-tuple-element.25), channel_id=1, source_target_pairs={{0,1016},{8,0},{16,8},{24,16},{32,24},{40,32},{48,40},{56,48},{64,... | collective-permute-start | bytes 124424 | tf_op jit(solution)/shard_map/ppermute | solution.py:34
  34.5 0.2 broadcast_in_dim.12.mass_ref
  34.8 0.2 broadcast_in_dim.13.potential_ref
  35.0 1.6 collective-permute-done.remote_ref
  36.6 1.3 shard_map.96
  37.9 1.9 collective-permute-start.1
  39.8 3.6 %shard_map.97.summed_ref = f32[1296,256]{1,0:T(8,128)S(1)} custom-call(bf16[1536,512]{1,0:T(8,128)(2,1)S(1)} %get-tuple-element.23.inner_ref, bf16[512,512]{1,0:T(8,128)(2,1)S(1)} %get-tuple-element.29.outer_ref, s32[24,128]{1,0:T(8,128)S(1)} %get-tuple-element.26.index_ref), custom_call_target="tpu_custom_call" | custom-call | flops 2700000000 | bytes 3000000 | tf_op jit(solution)/shard_map/pallas_call | solution.py:224
  43.5 9.2 %collective-permute-done.1.back_ref = bf16[81,256]{1,0:T(8,128)(2,1)S(1)} collective-permute-done((bf16[81,256]{1,0:T(8,128)(2,1)S(1)}, bf16[81,256]{1,0:T(8,128)(2,1)S(1)}, u32[]{:S(2)}, u32[]{:S(2)}) %collective-permute-start.1) | collective-permute-done | bytes 41504 | tf_op jit(solution)/shard_map/ppermute | solution.py:34
  52.6 0.8 shard_map.98
  53.5 3.7 %collective-permute-start.2 = (bf16[81,256]{1,0:T(8,128)(2,1)S(1)}, bf16[81,256]{1,0:T(8,128)(2,1)S(1)}, u32[]{:S(2)}, u32[]{:S(2)}) collective-permute-start(bf16[81,256]{1,0:T(8,128)(2,1)S(1)} %get-tuple-element.34), channel_id=1, source_target_pairs={{0,1016},{8,0},{16,8},{24,16},{32,24},{40,32},{48,40},{56,48},{64,... | collective-permute-start | bytes 124424 | tf_op jit(solution)/shard_map/ppermute | solution.py:34
  57.2 4.8 %shard_map.99 = (bf16[1536,512]{1,0:T(8,128)(2,1)S(1)}, bf16[512,256]{1,0:T(8,128)(2,1)S(1)}) custom-call(f32[16]{0:T(128)S(1)} %copy-done.6, bf16[1296,256]{1,0:T(8,128)(2,1)S(1)} %get-tuple-element.31.values_ref.middle_ref, s32[128,128]{1,0:T(8,128)S(1)} %get-tuple-element.27.index_t_ref, bf16[256,256]{1,0:T(8,128)(2,1)S(1)} %get-tuple-element.28.element_ref), custom_call_target="tpu_custom_call" | custom-call | flops 1600000000 | bytes 3000000 | tf_op jit(solution)/shard_map/pallas_call | solution.py:224
  62.0 1.3 shard_map.100
  63.3 2.3 %collective-permute-start.3 = (bf16[81,256]{1,0:T(8,128)(2,1)S(1)}, bf16[81,256]{1,0:T(8,128)(2,1)S(1)}, u32[]{:S(2)}, u32[]{:S(2)}) collective-permute-start(bf16[81,256]{1,0:T(8,128)(2,1)S(1)} %get-tuple-element.36), channel_id=1, source_target_pairs={{0,8},{8,16},{16,24},{24,32},{32,40},{40,48},{48,56},{56,64},{64,7... | collective-permute-start | bytes 124424 | tf_op jit(solution)/shard_map/ppermute | solution.py:34
  65.7 3.6 %shard_map.101.summed_ref = f32[1296,256]{1,0:T(8,128)S(1)} custom-call(bf16[1536,512]{1,0:T(8,128)(2,1)S(1)} %get-tuple-element.32.inner_ref, bf16[512,512]{1,0:T(8,128)(2,1)S(1)} %get-tuple-element.35.outer_ref, s32[24,128]{1,0:T(8,128)S(1)} %get-tuple-element.26.index_ref), custom_call_target="tpu_custom_call" | custom-call | flops 2700000000 | bytes 3000000 | tf_op jit(solution)/shard_map/pallas_call | solution.py:224
  69.3 8.3 %collective-permute-done.3.back_ref = bf16[81,256]{1,0:T(8,128)(2,1)S(1)} collective-permute-done((bf16[81,256]{1,0:T(8,128)(2,1)S(1)}, bf16[81,256]{1,0:T(8,128)(2,1)S(1)}, u32[]{:S(2)}, u32[]{:S(2)}) %collective-permute-start.3) | collective-permute-done | bytes 41504 | tf_op jit(solution)/shard_map/ppermute | solution.py:34
  77.6 1.7 shard_map.102
  79.3 1.9 collective-permute-start.4
  81.2 2.2 %collective-permute-start.6 = (bf16[1296,256]{1,0:T(8,128)(2,1)}, bf16[1296,256]{1,0:T(8,128)(2,1)S(1)}, u32[]{:S(2)}, u32[]{:S(2)}) collective-permute-start(bf16[1296,256]{1,0:T(8,128)(2,1)} %get-tuple-element.21), channel_id=1, source_target_pairs={{0,2},{2,4},{4,6},{1,3},{3,5},{5,7},{8,10},{10,12},{12,14},{9,11},... | collective-permute-start | bytes 1990664 | tf_op jit(solution)/shard_map/ppermute | solution.py:352
  83.4 3.8 %collective-permute-start.5 = (bf16[1296,256]{1,0:T(8,128)(2,1)}, bf16[1296,256]{1,0:T(8,128)(2,1)S(1)}, u32[]{:S(2)}, u32[]{:S(2)}) collective-permute-start(bf16[1296,256]{1,0:T(8,128)(2,1)} %get-tuple-element.21), channel_id=1, source_target_pairs={{2,0},{4,2},{6,4},{3,1},{5,3},{7,5},{10,8},{12,10},{14,12},{11,9},... | collective-permute-start | bytes 1990664 | tf_op jit(solution)/shard_map/ppermute | solution.py:352
  87.3 1.1 constant_dynamic-update-slice_fusion
  88.5 0.6 convolution_convert_fusion.3
  89.1 11.7 %collective-permute-done.6 = bf16[1296,256]{1,0:T(8,128)(2,1)S(1)} collective-permute-done((bf16[1296,256]{1,0:T(8,128)(2,1)}, bf16[1296,256]{1,0:T(8,128)(2,1)S(1)}, u32[]{:S(2)}, u32[]{:S(2)}) %collective-permute-start.6) | collective-permute-done | bytes 663584 | tf_op jit(solution)/shard_map/ppermute | solution.py:352
  100.8 1.9 collective-permute-done.5
  102.7 0.6 convolution_convert_fusion.2
  103.3 0.7 fusion.4
  104.0 2.3 %collective-permute-start.9 = (bf16[1296,256]{1,0:T(8,128)(2,1)S(1)}, bf16[1296,256]{1,0:T(8,128)(2,1)S(1)}, u32[]{:S(2)}, u32[]{:S(2)}) collective-permute-start(bf16[1296,256]{1,0:T(8,128)(2,1)S(1)} %collective-permute-done.6), channel_id=1, source_target_pairs={{2,4},{4,6},{3,5},{5,7},{10,12},{12,14},{11,13},{13,15},{18,20},{2... | collective-permute-start | bytes 1990664 | tf_op jit(solution)/shard_map/ppermute | solution.py:352
  106.3 2.1 %collective-permute-start.8 = (bf16[1296,256]{1,0:T(8,128)(2,1)S(1)}, bf16[1296,256]{1,0:T(8,128)(2,1)}, u32[]{:S(2)}, u32[]{:S(2)}) collective-permute-start(bf16[1296,256]{1,0:T(8,128)(2,1)S(1)} %collective-permute-done.5), channel_id=1, source_target_pairs={{2,0},{4,2},{3,1},{5,3},{10,8},{12,10},{11,9},{13,11},{18,16},{20,... | collective-permute-start | bytes 1990664 | tf_op jit(solution)/shard_map/ppermute | solution.py:352
  108.4 0.7 pad_maximum_fusion.1
  109.1 1.9 collective-permute-start.7
  111.0 1.8 collective-permute-done.7
  112.9 1.0 fusion.5
  113.9 1.0 pad_maximum_fusion
  114.8 0.9 copy.32
  115.7 4.2 %collective-permute-done.9 = bf16[1296,256]{1,0:T(8,128)(2,1)S(1)} collective-permute-done((bf16[1296,256]{1,0:T(8,128)(2,1)S(1)}, bf16[1296,256]{1,0:T(8,128)(2,1)S(1)}, u32[]{:S(2)}, u32[]{:S(2)}) %collective-permute-start.9) | collective-permute-done | bytes 663584 | tf_op jit(solution)/shard_map/ppermute | solution.py:352
  120.0 4.3 %collective-permute-done.8 = bf16[1296,256]{1,0:T(8,128)(2,1)} collective-permute-done((bf16[1296,256]{1,0:T(8,128)(2,1)S(1)}, bf16[1296,256]{1,0:T(8,128)(2,1)}, u32[]{:S(2)}, u32[]{:S(2)}) %collective-permute-start.8) | collective-permute-done | bytes 663584 | tf_op jit(solution)/shard_map/ppermute | solution.py:352
  124.2 2.0 broadcast_select_fusion.1
  126.2 2.1 %collective-permute-start.11 = (bf16[1296,256]{1,0:T(8,128)(2,1)}, bf16[1296,256]{1,0:T(8,128)(2,1)}, u32[]{:S(2)}, u32[]{:S(2)}) collective-permute-start(bf16[1296,256]{1,0:T(8,128)(2,1)} %broadcast_select_fusion.1), channel_id=1, source_target_pairs={{2,0},{4,6},{3,1},{5,7},{10,8},{12,14},{11,9},{13,15},{18,16},{20,... | collective-permute-start | bytes 1990664 | tf_op jit(solution)/shard_map/ppermute | solution.py:352
  128.4 0.2 select_select_fusion
  128.6 0.6 convolution_convert_fusion.1
  129.2 1.9 collective-permute-start.10
  131.1 3.5 %all-to-all-start = ((bf16[8,4,2,16,256]{4,3,2,1,0:T(8,128)(2,1)}), bf16[8,4,2,16,256]{4,3,2,1,0:T(8,128)(2,1)S(1)}, u32[]{:S(2)}, u32[]{:S(2)}) async-start(bf16[8,4,2,16,256]{4,3,2,1,0:T(8,128)(2,1)} %bitcast.8), calls=%async_computation | async-start | bytes 1048576 | tf_op jit(solution)/shard_map/all_to_all | solution.py:381
  134.7 0.7 copy.33
  135.4 5.2 %collective-permute-done.11 = bf16[1296,256]{1,0:T(8,128)(2,1)} collective-permute-done((bf16[1296,256]{1,0:T(8,128)(2,1)}, bf16[1296,256]{1,0:T(8,128)(2,1)}, u32[]{:S(2)}, u32[]{:S(2)}) %collective-permute-start.11) | collective-permute-done | bytes 663584 | tf_op jit(solution)/shard_map/ppermute | solution.py:352
  140.6 1.2 broadcast_select_fusion
  141.8 0.6 convolution_convert_fusion
  142.4 10.6 %all-to-all-done.first_ref = bf16[8,4,2,16,256]{4,3,2,1,0:T(8,128)(2,1)S(1)} async-done(((bf16[8,4,2,16,256]{4,3,2,1,0:T(8,128)(2,1)}), bf16[8,4,2,16,256]{4,3,2,1,0:T(8,128)(2,1)S(1)}, u32[]{:S(2)}, u32[]{:S(2)}) %all-to-all-start) | async-done | bytes 524320 | tf_op jit(solution)/shard_map/all_to_all | solution.py:381
  153.0 3.4 %all-to-all-start.1 = ((bf16[8,2,2,16,256]{4,3,2,1,0:T(8,128)(2,1)}), bf16[8,2,2,16,256]{4,3,2,1,0:T(8,128)(2,1)S(1)}, u32[]{:S(2)}, u32[]{:S(2)}) async-start(bf16[8,2,2,16,256]{4,3,2,1,0:T(8,128)(2,1)} %bitcast.13), calls=%async_computation.1 | async-start | bytes 524288 | tf_op jit(solution)/shard_map/all_to_all | solution.py:381
  156.5 2.0 collective-permute-start.12
  158.5 1.3 collective-permute-done.12
  159.8 0.7 copy.34
  160.5 8.3 %all-to-all-done.1.second_ref = bf16[8,2,2,16,256]{4,3,2,1,0:T(8,128)(2,1)S(1)} async-done(((bf16[8,2,2,16,256]{4,3,2,1,0:T(8,128)(2,1)}), bf16[8,2,2,16,256]{4,3,2,1,0:T(8,128)(2,1)S(1)}, u32[]{:S(2)}, u32[]{:S(2)}) %all-to-all-start.1) | async-done | bytes 262176 | tf_op jit(solution)/shard_map/all_to_all | solution.py:381
  168.8 3.4 %all-to-all-start.2 = ((bf16[8,2,2,16,256]{4,3,2,1,0:T(8,128)(2,1)}), bf16[8,2,2,16,256]{4,3,2,1,0:T(8,128)(2,1)S(1)}, u32[]{:S(2)}, u32[]{:S(2)}) async-start(bf16[8,2,2,16,256]{4,3,2,1,0:T(8,128)(2,1)} %bitcast.18), calls=%async_computation.2 | async-start | bytes 524288 | tf_op jit(solution)/shard_map/all_to_all | solution.py:381
  172.2 0.7 add_bitcast_fusion
  172.9 0.1 copy.23
  173.1 11.3 %all-to-all-done.2.third_ref = bf16[8,2,2,16,256]{4,3,2,1,0:T(8,128)(2,1)S(1)} async-done(((bf16[8,2,2,16,256]{4,3,2,1,0:T(8,128)(2,1)}), bf16[8,2,2,16,256]{4,3,2,1,0:T(8,128)(2,1)S(1)}, u32[]{:S(2)}, u32[]{:S(2)}) %all-to-all-start.2) | async-done | bytes 262176 | tf_op jit(solution)/shard_map/all_to_all | solution.py:381
  184.3 0.7 shard_map.103
  185.0 17.0 %all_to_all.20 = bf16[16,16,256]{2,1,0:T(8,128)(2,1)S(1)} all-to-all(bf16[16,16,256]{2,1,0:T(8,128)(2,1)S(1)} %bitcast.30), channel_id=1, replica_groups=mesh['xh'=2,'z'=8,'y'=8,'xl'=4,'c'=2] {'xh','z'}, dimensions={0} | all-to-all | bytes 262144 | tf_op jit(solution)/shard_map/all_to_all | solution.py:427
  202.0 0.6 convert_reduce_fusion
  (26 shorter events, 0.3 us)
Async XLA Ops:
  0.6 1.1 copy-start
  1.7 0.8 copy-start.2
  2.5 0.7 copy-start.3
  3.2 0.7 copy-start.4
  3.8 0.7 copy-start.5
  4.5 30.0 %copy-start.7 = (f32[1296]{0:T(1024)S(1)}, f32[1296]{0:T(1024)}, u32[]{:S(2)}) copy-start(f32[1296]{0:T(1024)} %param.13) | copy-start | bytes 15556
  4.5 30.3 %copy-start.8 = (f32[1296]{0:T(1024)S(1)}, f32[1296]{0:T(1024)}, u32[]{:S(2)}) copy-start(f32[1296]{0:T(1024)} %param.14) | copy-start | bytes 15556
  9.5 27.1 %collective-permute-start = (bf16[81,256]{1,0:T(8,128)(2,1)S(1)}, bf16[81,256]{1,0:T(8,128)(2,1)S(1)}, u32[]{:S(2)}, u32[]{:S(2)}) collective-permute-start(bf16[81,256]{1,0:T(8,128)(2,1)S(1)} %get-tuple-element.25), channel_id=1, source_target_pairs={{0,1016},{8,0},{16,8},{24,16},{32,24},{40,32},{48,40},{56,48},{64,... | collective-permute-start | bytes 124424 | tf_op jit(solution)/shard_map/ppermute | solution.py:34
  37.9 14.7 %collective-permute-start.1 = (bf16[81,256]{1,0:T(8,128)(2,1)S(1)}, bf16[81,256]{1,0:T(8,128)(2,1)S(1)}, u32[]{:S(2)}, u32[]{:S(2)}) collective-permute-start(bf16[81,256]{1,0:T(8,128)(2,1)S(1)} %get-tuple-element.30), channel_id=1, source_target_pairs={{0,8},{8,16},{16,24},{24,32},{32,40},{40,48},{48,56},{56,64},{64,7... | collective-permute-start | bytes 124424 | tf_op jit(solution)/shard_map/ppermute | solution.py:34
  39.8 12.8 %copy-start.1 = (bf16[1296,256]{1,0:T(8,128)(2,1)S(1)}, bf16[1296,256]{1,0:T(8,128)(2,1)}, u32[]{:S(2)}) copy-start(bf16[1296,256]{1,0:T(8,128)(2,1)} %values_ref.5) | copy-start | bytes 1990660
  43.5 13.7 %copy-start.6 = (f32[16]{0:T(128)S(1)}, f32[16]{0:T(128)}, u32[]{:S(2)}) copy-start(f32[16]{0:T(128)} %scale_ref.7) | copy-start | bytes 196
  53.5 8.6 %collective-permute-start.2 = (bf16[81,256]{1,0:T(8,128)(2,1)S(1)}, bf16[81,256]{1,0:T(8,128)(2,1)S(1)}, u32[]{:S(2)}, u32[]{:S(2)}) collective-permute-start(bf16[81,256]{1,0:T(8,128)(2,1)S(1)} %get-tuple-element.34), channel_id=1, source_target_pairs={{0,1016},{8,0},{16,8},{24,16},{32,24},{40,32},{48,40},{56,48},{64,... | collective-permute-start | bytes 124424 | tf_op jit(solution)/shard_map/ppermute | solution.py:34
  63.3 14.3 %collective-permute-start.3 = (bf16[81,256]{1,0:T(8,128)(2,1)S(1)}, bf16[81,256]{1,0:T(8,128)(2,1)S(1)}, u32[]{:S(2)}, u32[]{:S(2)}) collective-permute-start(bf16[81,256]{1,0:T(8,128)(2,1)S(1)} %get-tuple-element.36), channel_id=1, source_target_pairs={{0,8},{8,16},{16,24},{24,32},{32,40},{40,48},{48,56},{56,64},{64,7... | collective-permute-start | bytes 124424 | tf_op jit(solution)/shard_map/ppermute | solution.py:34
  79.3 8.0 %collective-permute-start.4 = (bf16[1296,256]{1,0:T(8,128)(2,1)S(1)}, bf16[1296,256]{1,0:T(8,128)(2,1)}, u32[]{:S(2)}, u32[]{:S(2)}) collective-permute-start(bf16[1296,256]{1,0:T(8,128)(2,1)S(1)} %get-tuple-element.38), channel_id=1, source_target_pairs={{0,1},{1,0},{2,3},{3,2},{4,5},{5,4},{6,7},{7,6},{8,9},{9,8},{10,11... | collective-permute-start | bytes 1990664 | tf_op jit(solution)/shard_map/ppermute | solution.py:352
  81.2 7.2 %copy-start.9 = (bf16[1296,256]{1,0:T(8,128)(2,1)S(1)}, bf16[1296,256]{1,0:T(8,128)(2,1)}, u32[]{:S(2)}) copy-start(bf16[1296,256]{1,0:T(8,128)(2,1)} %get-tuple-element.21) | copy-start | bytes 1990660
  81.2 19.5 %collective-permute-start.6 = (bf16[1296,256]{1,0:T(8,128)(2,1)}, bf16[1296,256]{1,0:T(8,128)(2,1)S(1)}, u32[]{:S(2)}, u32[]{:S(2)}) collective-permute-start(bf16[1296,256]{1,0:T(8,128)(2,1)} %get-tuple-element.21), channel_id=1, source_target_pairs={{0,2},{2,4},{4,6},{1,3},{3,5},{5,7},{8,10},{10,12},{12,14},{9,11},... | collective-permute-start | bytes 1990664 | tf_op jit(solution)/shard_map/ppermute | solution.py:352
  83.4 19.3 %collective-permute-start.5 = (bf16[1296,256]{1,0:T(8,128)(2,1)}, bf16[1296,256]{1,0:T(8,128)(2,1)S(1)}, u32[]{:S(2)}, u32[]{:S(2)}) collective-permute-start(bf16[1296,256]{1,0:T(8,128)(2,1)} %get-tuple-element.21), channel_id=1, source_target_pairs={{2,0},{4,2},{6,4},{3,1},{5,3},{7,5},{10,8},{12,10},{14,12},{11,9},... | collective-permute-start | bytes 1990664 | tf_op jit(solution)/shard_map/ppermute | solution.py:352
  104.0 15.9 %collective-permute-start.9 = (bf16[1296,256]{1,0:T(8,128)(2,1)S(1)}, bf16[1296,256]{1,0:T(8,128)(2,1)S(1)}, u32[]{:S(2)}, u32[]{:S(2)}) collective-permute-start(bf16[1296,256]{1,0:T(8,128)(2,1)S(1)} %collective-permute-done.6), channel_id=1, source_target_pairs={{2,4},{4,6},{3,5},{5,7},{10,12},{12,14},{11,13},{13,15},{18,20},{2... | collective-permute-start | bytes 1990664 | tf_op jit(solution)/shard_map/ppermute | solution.py:352
  106.3 17.9 %collective-permute-start.8 = (bf16[1296,256]{1,0:T(8,128)(2,1)S(1)}, bf16[1296,256]{1,0:T(8,128)(2,1)}, u32[]{:S(2)}, u32[]{:S(2)}) collective-permute-start(bf16[1296,256]{1,0:T(8,128)(2,1)S(1)} %collective-permute-done.5), channel_id=1, source_target_pairs={{2,0},{4,2},{3,1},{5,3},{10,8},{12,10},{11,9},{13,11},{18,16},{20,... | collective-permute-start | bytes 1990664 | tf_op jit(solution)/shard_map/ppermute | solution.py:352
  109.1 3.8 %collective-permute-start.7 = (bf16[512,256]{1,0:T(8,128)(2,1)}, bf16[512,256]{1,0:T(8,128)(2,1)}, u32[]{:S(2)}, u32[]{:S(2)}) collective-permute-start(bf16[512,256]{1,0:T(8,128)(2,1)} %pad_maximum_fusion.1), channel_id=1, source_target_pairs={{0,1},{1,0},{2,3},{3,2},{4,5},{5,4},{6,7},{7,6},{8,9},{9,8},{10,11... | collective-permute-start | bytes 786440 | tf_op jit(solution)/shard_map/ppermute | solution.py:352
  126.2 14.4 %collective-permute-start.11 = (bf16[1296,256]{1,0:T(8,128)(2,1)}, bf16[1296,256]{1,0:T(8,128)(2,1)}, u32[]{:S(2)}, u32[]{:S(2)}) collective-permute-start(bf16[1296,256]{1,0:T(8,128)(2,1)} %broadcast_select_fusion.1), channel_id=1, source_target_pairs={{2,0},{4,6},{3,1},{5,7},{10,8},{12,14},{11,9},{13,15},{18,16},{20,... | collective-permute-start | bytes 1990664 | tf_op jit(solution)/shard_map/ppermute | solution.py:352
  129.2 5.4 %collective-permute-start.10 = (bf16[256,256]{1,0:T(8,128)(2,1)S(1)}, bf16[256,256]{1,0:T(8,128)(2,1)S(1)}, u32[]{:S(2)}, u32[]{:S(2)}) collective-permute-start(bf16[256,256]{1,0:T(8,128)(2,1)S(1)} %get-tuple-element.47), channel_id=1, source_target_pairs={{0,1},{1,0},{2,3},{3,2},{4,5},{5,4},{6,7},{7,6},{8,9},{9,8},{10,11... | collective-permute-start | bytes 393224 | tf_op jit(solution)/shard_map/ppermute | solution.py:352
  131.1 21.9 %all-to-all-start = ((bf16[8,4,2,16,256]{4,3,2,1,0:T(8,128)(2,1)}), bf16[8,4,2,16,256]{4,3,2,1,0:T(8,128)(2,1)S(1)}, u32[]{:S(2)}, u32[]{:S(2)}) async-start(bf16[8,4,2,16,256]{4,3,2,1,0:T(8,128)(2,1)} %bitcast.8), calls=%async_computation | async-start | bytes 1048576 | tf_op jit(solution)/shard_map/all_to_all | solution.py:381
  153.0 15.7 %all-to-all-start.1 = ((bf16[8,2,2,16,256]{4,3,2,1,0:T(8,128)(2,1)}), bf16[8,2,2,16,256]{4,3,2,1,0:T(8,128)(2,1)S(1)}, u32[]{:S(2)}, u32[]{:S(2)}) async-start(bf16[8,2,2,16,256]{4,3,2,1,0:T(8,128)(2,1)} %bitcast.13), calls=%async_computation.1 | async-start | bytes 524288 | tf_op jit(solution)/shard_map/all_to_all | solution.py:381
  156.5 3.2 %collective-permute-start.12 = (bf16[256,256]{1,0:T(8,128)(2,1)S(1)}, bf16[256,256]{1,0:T(8,128)(2,1)S(1)}, u32[]{:S(2)}, u32[]{:S(2)}) collective-permute-start(bf16[256,256]{1,0:T(8,128)(2,1)S(1)} %get-tuple-element.45), channel_id=1, source_target_pairs={{0,1},{1,0},{2,3},{3,2},{4,5},{5,4},{6,7},{7,6},{8,9},{9,8},{10,11... | collective-permute-start | bytes 393224 | tf_op jit(solution)/shard_map/ppermute | solution.py:352
  168.8 15.6 %all-to-all-start.2 = ((bf16[8,2,2,16,256]{4,3,2,1,0:T(8,128)(2,1)}), bf16[8,2,2,16,256]{4,3,2,1,0:T(8,128)(2,1)S(1)}, u32[]{:S(2)}, u32[]{:S(2)}) async-start(bf16[8,2,2,16,256]{4,3,2,1,0:T(8,128)(2,1)} %bitcast.18), calls=%async_computation.2 | async-start | bytes 524288 | tf_op jit(solution)/shard_map/all_to_all | solution.py:381
